TPU v7x, 32 devices: a whole 2x2x4 slice. The times are simulated.
32 devices in a mesh: fsdp: 4 (over x, core), context: 4 (over z), tensor: 2 (over y).
Axes of the slice: x: 2, y: 2, z: 4, core: 2. Of those that a mesh axis runs over, the one named last changes fastest.
Arguments:
- block_input: float32 [8192, 768], P(('fsdp', 'context')), may hold values from -18 to 18
- ln1_gain: float32 [768], replicated, may hold values from 0.1 to 1.9
- ln1_shift: float32 [768], replicated, may hold values from -3 to 3
- qkv_weight: float32 [768, 3, 768], P(('fsdp', 'context'), None, 'tensor'), may hold values from -0.21875 to 0.21875
- qkv_bias: float32 [3, 768], P(None, 'tensor'), may hold values from -3 to 3
- feat_query: float32 [12, 64, 64], P('tensor'), may hold values from -1.5 to 1.5
- feat_key: float32 [12, 64, 64], P('tensor'), may hold values from -1.5 to 1.5
- out_weight: float32 [768, 768], P('tensor', ('fsdp', 'context')), may hold values from -3.5 to 3.5
- out_bias: float32 [768], replicated, may hold values from -3 to 3
- ln2_gain: float32 [768], replicated, may hold values from 0.1 to 1.9
- ln2_shift: float32 [768], replicated, may hold values from -3 to 3
- up_weight: float32 [768, 3072], P(('fsdp', 'context'), 'tensor'), may hold values from -0.21875 to 0.21875
- up_bias: float32 [3072], P('tensor'), may hold values from -3 to 3
- down_weight: float32 [3072, 768], P('tensor', ('fsdp', 'context')), may hold values from -0.109375 to 0.109375
- down_bias: float32 [768], replicated, may hold values from -3 to 3
- lengths: int32 [4], replicated, may hold values from 1024 to 2048, as said below
- deal: int32 [128], P(('fsdp', 'context')), may hold values from 0 to 127, as said below
- cotangent: float32 [8192, 768], P(('fsdp', 'context')), may hold values from -6 to 6
Outputs:
- dealt_output: float32 [128, 64, 768], P(('fsdp', 'context'), 'tensor')
- rms: float32 [3], replicated
- grad_input: float32 [8192, 768], P(('fsdp', 'context'))
- grad_ln1_gain: float32 [768], replicated
- grad_ln1_shift: float32 [768], replicated
- grad_qkv_weight: float32 [768, 3, 768], P(('fsdp', 'context'), None, 'tensor')
- grad_qkv_bias: float32 [3, 768], P(None, 'tensor')
- grad_feat_query: float32 [12, 64, 64], P('tensor')
- grad_feat_key: float32 [12, 64, 64], P('tensor')
- grad_out_weight: float32 [768, 768], P('tensor', ('fsdp', 'context'))
- grad_out_bias: float32 [768], replicated
- grad_ln2_gain: float32 [768], replicated
- grad_ln2_shift: float32 [768], replicated
- grad_up_weight: float32 [768, 3072], P(('fsdp', 'context'), 'tensor')
- grad_up_bias: float32 [3072], P('tensor')
- grad_down_weight: float32 [3072, 768], P('tensor', ('fsdp', 'context'))
- grad_down_bias: float32 [768], replicated
Inputs may be any that keep to these rules, and one draw needn't show every extreme that they name: Sequence lengths; the 4 lengths sum to exactly 8160, and the last of them is exactly 2048. deal is a permutation of the 128 groups. Group j of the device with fsdp index f and context index e (groups numbered along fsdp, then context, then position) goes to position (f * 4 + d) * 8 + e * 2 + r, where the 8 groups of one device take every pair of d < 4 and r < 2 once.
All inputs are finite; a program needn't handle non-finite values.
Results may differ from a plain program's by a relative error of at most 0.0003.
Values sent between devices are 32-bit elements; how exact they have to be, the bound alone decides.
No kernel may reach another device: no remote copies, remote signals or barrier semaphores. Data moves between devices by JAX's collectives and lax.ppermute only.
A program may use at most 128 MiB of HBM per device.

v0:
```python
from functools import partial

import jax
import jax.numpy as jnp
from jax import lax
from jax.sharding import PartitionSpec as P

HIGH = lax.Precision.HIGHEST
NORM_EPS = 1e-05


def entering(x, axis, combine, identity, reverse):
    count, place = (lax.axis_size(axis), lax.axis_index(axis))
    everything = jax.tree.map(lambda part: lax.all_gather(part, axis), x)
    start = jax.tree.map(
        lambda part, zero: jnp.broadcast_to(jnp.asarray(zero, part.dtype), part.shape), x, identity
    )

    def lap(k, before):
        at = count - 1 - k if reverse else k
        reached = at > place if reverse else at < place
        new = combine(before, jax.tree.map(lambda part: part[at], everything))
        return jax.tree.map(lambda a, b: jnp.where(reached, a, b), new, before)

    return lax.fori_loop(0, count, lap, start)


def layer_norm(values, gain, shift):
    middle = jnp.mean(values, axis=-1, keepdims=True)
    centred = values - middle
    spread = jnp.mean(centred * centred, axis=-1, keepdims=True)
    return centred * lax.rsqrt(spread + NORM_EPS) * gain + shift


def feature_map(heads, weight):
    logits = jnp.einsum("rhd,hde->rhe", heads, weight, precision=HIGH)
    return jnp.concatenate(
        [jax.nn.softmax(logits, axis=-1), jax.nn.softmax(-logits, axis=-1)], axis=-1
    )


def segment_of(places, ends, total, number):
    found = jnp.sum((ends[None, :] <= places[:, None]).astype(jnp.int32), axis=1)
    found = jnp.where(places < 0, -1, found)
    return jnp.where(places >= total, number + 1, found)


def project(normed, weight, bias):
    return jnp.einsum("rd,dke->rke", normed, weight, precision=HIGH) + bias


def mlp_part(normed, up_full, up_bias, down_full):
    active = jax.nn.gelu(jnp.dot(normed, up_full, precision=HIGH) + up_bias, approximate=True)
    return jnp.dot(active, down_full, precision=HIGH)


def chain_join(earlier, later):
    passing = 1.0 - later[2]
    return (
        later[0] + passing * earlier[0],
        later[1] + passing * earlier[1],
        jnp.maximum(earlier[2], later[2]),
    )


def local_part(queries, keys, values, weight_q, weight_k, segment, seg_first, block):
    phi_q = feature_map(queries, weight_q)
    phi_k = feature_map(keys, weight_k)
    count_rows, local_heads, head_dim = values.shape
    feats = phi_q.shape[2]
    blocks = count_rows // block
    lower = jnp.arange(block)[:, None] >= jnp.arange(block)[None, :]

    def block_step(carry, pieces):
        state, normer, seg_carry = carry
        piece_q, piece_k, piece_v, seg_piece = pieces
        allowed = jnp.logical_and(lower, seg_piece[:, None] == seg_piece[None, :]).astype(
            jnp.float32
        )
        scores = jnp.einsum("ihf,jhf->hij", piece_q, piece_k, precision=HIGH) * allowed[None]
        numer = jnp.einsum("hij,jhd->ihd", scores, piece_v, precision=HIGH)
        denom = jnp.einsum("hij->ih", scores)
        carried = (seg_piece == seg_carry).astype(jnp.float32)
        numer = numer + carried[:, None, None] * jnp.einsum(
            "ihf,hfd->ihd", piece_q, state, precision=HIGH
        )
        denom = denom + carried[:, None] * jnp.einsum("ihf,hf->ih", piece_q, normer, precision=HIGH)
        final_seg = seg_piece[-1]
        stays = (final_seg == seg_carry).astype(jnp.float32)
        tail_k = piece_k * (seg_piece == final_seg).astype(jnp.float32)[:, None, None]
        state = stays * state + jnp.einsum("jhf,jhd->hfd", tail_k, piece_v, precision=HIGH)
        normer = stays * normer + jnp.sum(tail_k, axis=0)
        return ((state, normer, final_seg), (numer, denom))

    def blocked(array):
        return array.reshape((blocks, block) + array.shape[1:])

    start = (
        jnp.zeros((local_heads, feats, head_dim), jnp.float32),
        jnp.zeros((local_heads, feats), jnp.float32),
        seg_first,
    )
    (state, normer, _), (numer, denom) = lax.scan(
        jax.checkpoint(block_step),
        start,
        (blocked(phi_q), blocked(phi_k), blocked(values), blocked(segment)),
    )
    return (
        phi_q,
        numer.reshape(count_rows, local_heads, head_dim),
        denom.reshape(count_rows, local_heads),
        state,
        normer,
    )


def body(
    block_input,
    ln1_gain,
    ln1_shift,
    qkv_weight,
    qkv_bias,
    feat_query,
    feat_key,
    out_weight,
    out_bias,
    ln2_gain,
    ln2_shift,
    up_weight,
    up_bias,
    down_weight,
    down_bias,
    lengths,
    deal,
    cotangent,
):
    count_rows, width = block_input.shape
    local_heads, head_dim = (feat_query.shape[0], feat_query.shape[1])
    local_width = local_heads * head_dim
    offset = lax.axis_index(("fsdp", "context")) * count_rows
    total = count_rows * lax.axis_size(("fsdp", "context"))
    ends = jnp.cumsum(lengths)
    used = ends[-1]
    number = lengths.shape[0]
    places = offset + jnp.arange(count_rows, dtype=jnp.int32)
    segment = segment_of(places, ends, total, number)
    edges = segment_of(offset + jnp.array([-1, count_rows], dtype=jnp.int32), ends, total, number)
    seg_first = segment[0]
    seg_final = segment[-1]
    carry_in = (edges[0] == seg_first).astype(jnp.float32)
    breaks = (edges[0] != seg_final).astype(jnp.float32)
    valid = (places < used).astype(jnp.float32)[:, None]
    block = min(512, count_rows)
    qkv_full, out_full, up_full, down_full = (
        lax.all_gather(qkv_weight, ("fsdp", "context"), axis=0, tiled=True),
        lax.all_gather(out_weight, ("fsdp", "context"), axis=1, tiled=True),
        lax.all_gather(up_weight, ("fsdp", "context"), axis=0, tiled=True),
        lax.all_gather(down_weight, ("fsdp", "context"), axis=1, tiled=True),
    )
    normed1 = layer_norm(block_input, ln1_gain, ln1_shift)
    qkv = project(normed1, qkv_full, qkv_bias)
    queries = qkv[:, 0, :].reshape(count_rows, local_heads, head_dim)
    keys = qkv[:, 1, :].reshape(count_rows, local_heads, head_dim)
    values = qkv[:, 2, :].reshape(count_rows, local_heads, head_dim)
    attend_local = partial(local_part, segment=segment, seg_first=seg_first, block=block)
    phi_q, numer_local, denom_local, state_tail, norm_tail = attend_local(
        queries, keys, values, feat_query, feat_key
    )
    identity = (jnp.zeros_like(state_tail), jnp.zeros_like(norm_tail), jnp.zeros((), jnp.float32))
    state_scan, norm_scan, _ = entering(
        (state_tail, norm_tail, breaks), ("fsdp", "context"), chain_join, identity, False
    )
    state_in = carry_in * state_scan
    norm_in = carry_in * norm_scan
    first_rows = (segment == seg_first).astype(jnp.float32)[:, None, None]
    masked_q = phi_q * first_rows
    numer = numer_local + jnp.einsum("rhf,hfd->rhd", masked_q, state_in, precision=HIGH)
    denom = denom_local + jnp.einsum("rhf,hf->rh", masked_q, norm_in, precision=HIGH)
    attended = numer / denom[:, :, None]
    attended_flat = attended.reshape(count_rows, local_width)
    attn_part = jnp.dot(attended_flat, out_full, precision=HIGH)
    attn = lax.psum(attn_part, "tensor") + out_bias
    hidden = block_input + attn
    normed2 = layer_norm(hidden, ln2_gain, ln2_shift)
    slots = deal.shape[0]
    group_rows = count_rows // slots
    part_rows = group_rows // lax.axis_size("tensor")
    part_start = lax.axis_index("tensor") * part_rows
    per_peer = slots // lax.axis_size("context")
    slot_of = deal // slots % lax.axis_size("context") * per_peer + deal % per_peer
    counting = jnp.arange(slots, dtype=jnp.int32)
    source_of = jnp.sum(
        jnp.where(slot_of[None, :] == counting[:, None], counting[None, :], 0), axis=1
    )
    mlp_terms = mlp_part(normed2, up_full, up_bias, down_full)
    mlp = lax.psum(mlp_terms, "tensor") + down_bias
    result = hidden + mlp
    outbound = jnp.take(result.reshape(slots, group_rows, width), source_of, axis=0)
    dealt_whole = lax.all_to_all(outbound, "context", split_axis=0, concat_axis=0, tiled=True)
    dealt_output = lax.dynamic_slice_in_dim(dealt_whole, part_start, part_rows, 1)
    squares = jnp.stack(
        [jnp.sum(valid * result * result), jnp.sum(valid * attn * attn), jnp.sum(valid * mlp * mlp)]
    )
    inbound = lax.all_to_all(
        cotangent.reshape(slots, group_rows, width),
        "context",
        split_axis=0,
        concat_axis=0,
        tiled=True,
    )
    grad_y = jnp.take(inbound, slot_of, axis=0).reshape(count_rows, width) * valid
    grad_down_bias = jnp.sum(grad_y, axis=0)
    _, mlp_backward = jax.vjp(mlp_part, normed2, up_full, up_bias, down_full)
    grad_normed2_part, grad_up_full, grad_up_bias, grad_down_full = mlp_backward(grad_y)
    grad_normed2 = lax.psum(grad_normed2_part, "tensor")
    _, norm2_backward = jax.vjp(layer_norm, hidden, ln2_gain, ln2_shift)
    grad_hidden_norm, grad_ln2_gain, grad_ln2_shift = norm2_backward(grad_normed2)
    grad_hidden = grad_y + grad_hidden_norm
    grad_out_bias = jnp.sum(grad_hidden, axis=0)
    grad_out_full = jnp.einsum("rd,re->de", attended_flat, grad_hidden, precision=HIGH)
    grad_attended = jnp.einsum("re,de->rd", grad_hidden, out_full, precision=HIGH).reshape(
        count_rows, local_heads, head_dim
    )
    grad_numer = grad_attended / denom[:, :, None]
    grad_denom = -jnp.sum(grad_attended * attended, axis=2) / denom
    grad_state_in = carry_in * jnp.einsum("rhf,rhd->hfd", masked_q, grad_numer, precision=HIGH)
    grad_norm_in = carry_in * jnp.einsum("rhf,rh->hf", masked_q, grad_denom, precision=HIGH)
    grad_phi_extra = first_rows * (
        jnp.einsum("rhd,hfd->rhf", grad_numer, state_in, precision=HIGH)
        + grad_denom[:, :, None] * norm_in[None, :, :]
    )
    grad_state_tail, grad_norm_tail, _ = entering(
        (grad_state_in, grad_norm_in, breaks), ("fsdp", "context"), chain_join, identity, True
    )
    _, attention_backward = jax.vjp(attend_local, queries, keys, values, feat_query, feat_key)
    grad_queries, grad_keys, grad_values, grad_feat_query, grad_feat_key = attention_backward(
        (grad_phi_extra, grad_numer, grad_denom, grad_state_tail, grad_norm_tail)
    )
    grad_qkv = jnp.stack(
        [
            grad_queries.reshape(count_rows, local_width),
            grad_keys.reshape(count_rows, local_width),
            grad_values.reshape(count_rows, local_width),
        ],
        axis=1,
    )
    _, project_backward = jax.vjp(project, normed1, qkv_full, qkv_bias)
    grad_normed1_part, grad_qkv_full, grad_qkv_bias = project_backward(grad_qkv)
    grad_normed1 = lax.psum(grad_normed1_part, "tensor")
    _, norm1_backward = jax.vjp(layer_norm, block_input, ln1_gain, ln1_shift)
    grad_input_norm, grad_ln1_gain, grad_ln1_shift = norm1_backward(grad_normed1)
    grad_input = grad_hidden + grad_input_norm
    grad_qkv_weight, grad_out_weight, grad_up_weight, grad_down_weight = (
        lax.psum_scatter(grad_qkv_full, ("fsdp", "context"), scatter_dimension=0, tiled=True),
        lax.psum_scatter(grad_out_full, ("fsdp", "context"), scatter_dimension=1, tiled=True),
        lax.psum_scatter(grad_up_full, ("fsdp", "context"), scatter_dimension=0, tiled=True),
        lax.psum_scatter(grad_down_full, ("fsdp", "context"), scatter_dimension=1, tiled=True),
    )
    summed = lax.psum(
        (
            grad_ln1_gain,
            grad_ln1_shift,
            grad_qkv_bias,
            grad_feat_query,
            grad_feat_key,
            grad_out_bias,
            grad_ln2_gain,
            grad_ln2_shift,
            grad_up_bias,
            grad_down_bias,
            squares,
        ),
        ("fsdp", "context"),
    )
    rms = jnp.sqrt(summed[10] / (used.astype(jnp.float32) * width))
    return (
        dealt_output,
        rms,
        grad_input,
        summed[0],
        summed[1],
        grad_qkv_weight,
        summed[2],
        summed[3],
        summed[4],
        grad_out_weight,
        summed[5],
        summed[6],
        summed[7],
        grad_up_weight,
        summed[8],
        grad_down_weight,
        summed[9],
    )


def solution(mesh):
    in_specs = (
        P(("fsdp", "context"), None),
        P(),
        P(),
        P(("fsdp", "context"), None, "tensor"),
        P(None, "tensor"),
        P("tensor", None, None),
        P("tensor", None, None),
        P("tensor", ("fsdp", "context")),
        P(),
        P(),
        P(),
        P(("fsdp", "context"), "tensor"),
        P("tensor"),
        P("tensor", ("fsdp", "context")),
        P(),
        P(),
        P(("fsdp", "context")),
        P(("fsdp", "context"), None),
    )
    out_specs = (
        P(("fsdp", "context"), "tensor", None),
        P(),
        P(("fsdp", "context"), None),
        P(),
        P(),
        P(("fsdp", "context"), None, "tensor"),
        P(None, "tensor"),
        P("tensor", None, None),
        P("tensor", None, None),
        P("tensor", ("fsdp", "context")),
        P(),
        P(),
        P(),
        P(("fsdp", "context"), "tensor"),
        P("tensor"),
        P("tensor", ("fsdp", "context")),
        P(),
    )
    return jax.shard_map(body, mesh=mesh, in_specs=in_specs, out_specs=out_specs, check_vma=False)
```

profile of v0, /device:TPU:0, one launch (start us, length us, event | category | flops | bytes accessed | tf_op | source)
XLA Modules:
  0.0 1227.2 jit_solution(8723379923862665840)
XLA Ops:
  13.2 47.0 %all-gather.13.cloned.1.call-done = f32[768,3,384]{2,0,1:T(8,128)} async-done(((f32[48,3,384]{2,0,1:T(8,128)}), f32[768,3,384]{2,0,1:T(8,128)}) %all-gather.13.cloned.1.call-update) | async-done | bytes 3538960 | tf_op jit(solution)/shard_map/all_gather | solution.py:155
  60.3 8.5 convolution_add_fusion.1
  74.2 2.6 fusion.35
  82.2 43.4 %all-reduce = f32[16]{0:T(128)} all-reduce(f32[16]{0:T(128)S(1)} %dynamic-update-slice), channel_id=1, replica_groups=mesh['fsdp'=4,'context'=4,'tensor'=2] {'fsdp','context'}, use_global_device_ids=true, to_apply=%add | all-reduce | flops 16 | bytes 128
  130.5 31.8 %all-gather.4 = f32[16,6,128]{2,1,0:T(8,128)} all-gather(f32[1,6,128]{2,1,0:T(8,128)S(1)} %bitcast.196), channel_id=3, replica_groups=mesh['fsdp'=4,'context'=4,'tensor'=2] {'fsdp','context'}, dimensions={0}, use_global_device_ids=true | all-gather | bytes 52224 | tf_op jit(solution)/shard_map/all_gather | solution.py:14
  165.9 8.0 multiply_reduce_fusion
  174.0 111.7 %while.22 = (s32[]{:T(128)}, f32[6,128,64]{2,1,0:T(8,128)}, f32[6,128]{1,0:T(8,128)}, s32[]{:T(128)}, f32[16,6,128,64]{2,3,1,0:T(8,128)}, /*index=5*/f32[16]{0:T...) while((s32[]{:T(128)}, f32[6,128,64]{2,1,0:T(8,128)}, f32[6,128]{1,0:T(8,128)}, ...), condition=%wide.region_15.16_spmd.clone, body=%wide.region_14.15_spmd.clone.sunk | while | flops 199685 | bytes 1385643 | solution.py:25
  184.6 1.9 fusion.217
  191.6 1.9 fusion.217
  205.6 1.9 fusion.217
  226.5 1.9 fusion.217
  233.5 1.9 fusion.217
  240.5 1.9 fusion.217
  254.5 1.9 fusion.217
  261.5 1.9 fusion.217
  268.5 1.9 fusion.217
  282.5 1.9 fusion.217
  290.9 6.3 fusion.59
  297.2 6.6 fusion.167
  304.4 3.6 all-to-all-start.1
  310.1 33.8 %all-to-all-done.1 = f32[8,64,768]{2,1,0:T(8,128)S(1)} async-done(((f32[8,64,768]{2,1,0:T(8,128)}), f32[8,64,768]{2,1,0:T(8,128)S(1)}, u32[]{:S(2)}, u32[]{:S(2)}) %all-to-all-start.1) | async-done | bytes 1572896 | tf_op jit(solution)/shard_map/all_to_all | solution.py:204
  345.7 2.2 multiply_reduce_fusion.1
  349.3 11.4 fusion.168
  362.8 47.3 %all-gather.17.cloned.1.call-done = f32[768,1536]{1,0:T(8,128)} async-done(((f32[48,1536]{1,0:T(8,128)}), f32[768,1536]{1,0:T(8,128)}) %all-gather.17.cloned.1.call-update) | async-done | bytes 4718608 | tf_op jit(solution)/shard_map/all_gather | solution.py:157
  410.1 14.9 %fusion.155 = (f32[1536]{0:T(1024)}, f32[512,1536]{1,0:T(8,128)S(1)}, f32[512,1536]{1,0:T(8,128)}) fusion(f32[512,1536]{1,0:T(8,128)} %fusion.168, f32[1536]{0:T(1024)S(1)} %copy-done.118, f32[768,1536]{1,0:T(8,128)} %all-gather.17.cloned.1.call-done, f32[512,768]{1,0:T(8,128)S(1)} %get-tuple-element.631, f32[768]{0:T(1024)S(1)} %copy-done.83, ...), kind=kOutput, calls=%fused_computation.257 | convolution fusion | flops 7265843712 | bytes 15751168 | tf_op jit(solution)/shard_map/dot_general | solution.py:53
  426.6 9.0 fusion.169
  435.9 50.0 %all-reduce.11.cloned.1.call-done = f32[512,768]{1,0:T(8,128)} async-done(((f32[512,768]{1,0:T(8,128)}), f32[512,768]{1,0:T(8,128)}) %all-reduce.11.cloned.1.call-update) | async-done | bytes 1572880 | tf_op jit(solution)/shard_map/psum | solution.py:215
  485.9 2.7 multiply_reduce_fusion.2
  491.4 2.2 fusion.170
  495.3 2.6 fusion.71
  498.8 2.9 pad_maximum_fusion.1
  503.5 12.7 %fusion.38 = f32[512,768]{1,0:T(8,128)} fusion(f32[1536,768]{0,1:T(8,128)} %all-gather.19.cloned.1.call-done, f32[512,1536]{1,0:T(8,128)S(1)} %copy-done.124), kind=kOutput, calls=%fused_computation.80 | convolution fusion | flops 7254048768 | bytes 9437184 | tf_op jit(solution)/shard_map/dot_general | solution.py:54
  517.7 35.5 %all-gather.5 = f32[16,6,128]{2,1,0:T(8,128)} all-gather(f32[1,6,128]{2,1,0:T(8,128)S(1)} %fusion.126), channel_id=5, replica_groups=mesh['fsdp'=4,'context'=4,'tensor'=2] {'fsdp','context'}, dimensions={0}, use_global_device_ids=true | all-gather | bytes 52224 | tf_op jit(solution)/shard_map/all_gather | solution.py:14
  553.3 111.7 %while.23 = (s32[]{:T(128)}, f32[6,128,64]{2,1,0:T(8,128)}, f32[6,128]{1,0:T(8,128)}, s32[]{:T(128)}, f32[16,6,128,64]{2,3,1,0:T(8,128)}, /*index=5*/f32[16]{0:T...) while((s32[]{:T(128)}, f32[6,128,64]{2,1,0:T(8,128)}, ...), condition=%wide.region_31.33_spmd.clone, body=%wide.region_30.32_spmd.clone.sunk | while | flops 199689 | bytes 1385705 | solution.py:25
  666.2 2.2 and_convert_fusion
  668.4 2.6 copy.110
  671.0 7.3 fusion.171
  678.4 5.1 fusion.88
  683.6 5.3 fusion.12
  688.9 8.5 fusion.13
  697.4 4.1 fusion.8
  702.8 2.0 fusion.47
  704.8 2.3 copy.118
  707.1 3.3 bitcast_add_fusion.4
  714.2 2.3 copy.117
  716.6 2.7 fusion.90
  725.2 2.3 copy.116
  727.5 10.4 convolution_bitcast_fusion
  738.0 5.4 fusion.172
  743.5 12.1 fusion.62
  755.6 12.1 fusion.37
  767.9 3.0 fusion.83
  772.7 10.1 fusion.30
  783.6 37.0 %all-reduce.15.cloned.1.call-done = (f32[512,768]{1,0:T(8,128)}, f32[512,768]{1,0:T(8,128)}) async-done(((f32[512,768]{1,0:T(8,128)}, f32[512,768]{1,0:T(8,128)}), (f32[512,768]{1,0:T(8,128)}, f32[512,768]{1,0:T(8,128)})) %all-reduce.15.cloned.1.call-update) | async-done | bytes 3145744 | tf_op jit(solution)/shard_map/psum | solution.py:196
  820.6 4.1 fusion.26
  824.7 2.1 gather_fusion
  828.1 4.7 all-to-all-start
  835.0 2.0 pad_maximum_fusion.5
  837.8 89.3 %all-reduce.1 = (f32[3]{0:T(128)S(1)}, f32[768]{0:T(1024)}, f32[768]{0:T(1024)}, f32[3,384]{1,0:T(4,128)}, f32[768]{0:T(1024)}, /*index=5*/f32[768]{0:T(1024)}, f32[768]{0:T(1024)}, f32[1536]{0:T(1024)}, f32[768]{0:T(1024)}) all-reduce(f32[3]{0:T(128)S(1)} %pad_maximum_fusion.5, ...), channel_id=1, replica_groups=mesh['fsdp'=4,'context'=4,'tensor'=2] {'fsdp','context'}, use_global_device_ids=true, to_apply=%region_25.27 | all-reduce | flops 7299 | bytes 58392 | tf_op jit(solution)/shard_map/psum | solution.py:259
  930.3 2.1 constant_dynamic-slice_fusion.2
  932.4 38.8 %reduce-scatter.9.cloned.1.call-done = f32[48,1536]{1,0:T(8,128)} async-done(((f32[768,1536]{1,0:T(8,128)}), f32[48,1536]{1,0:T(8,128)}) %reduce-scatter.9.cloned.1.call-update) | async-done | bytes 294928 | tf_op jit(solution)/shard_map/reduce_scatter | solution.py:256
  971.2 79.1 %reduce-scatter.11.cloned.1.call-done = f32[1536,48]{0,1:T(8,128)} async-done(((f32[1536,768]{0,1:T(8,128)}), f32[1536,48]{0,1:T(8,128)}) %reduce-scatter.11.cloned.1.call-update) | async-done | bytes 294928 | tf_op jit(solution)/shard_map/reduce_scatter | solution.py:257
  1050.3 95.4 %all-reduce.13.cloned.1.call-done = (f32[6,64,64]{2,1,0:T(8,128)}, f32[6,64,64]{2,1,0:T(8,128)}) async-done(((f32[6,64,64]{2,1,0:T(8,128)}, f32[6,64,64]{2,1,0:T(8,128)}), (f32[6,64,64]{2,1,0:T(8,128)}, f32[6,64,64]{2,1,0:T(8,128)})) %all-reduce.13.cloned.1.call-update) | async-done | bytes 196624 | tf_op jit(solution)/shard_map/psum | solution.py:259
  1145.7 71.5 %reduce-scatter.5.cloned.1.call-done = f32[48,3,384]{2,0,1:T(8,128)} async-done(((f32[768,3,384]{2,0,1:T(8,128)}), f32[48,3,384]{2,0,1:T(8,128)}) %reduce-scatter.5.cloned.1.call-update) | async-done | bytes 221200 | tf_op jit(solution)/shard_map/reduce_scatter | solution.py:254
  (528 shorter events, 254.5 us)
Async XLA Ops:
  7.2 62.7 %copy-start = (f32[6,64,64]{2,1,0:T(8,128)S(1)}, f32[6,64,64]{2,1,0:T(8,128)}, u32[]{:S(2)}) copy-start(f32[6,64,64]{2,1,0:T(8,128)} %param.31) | copy-start | bytes 294916
  7.2 53.1 %all-gather.13.cloned.1.call-start = ((), (), s32[]{:S(2)}) async-start(), calls=%async_computation.6 | async-start | bytes 3760128 | tf_op jit(solution)/shard_map/all_gather | solution.py:155
  8.0 166.0 %all-gather.21.cloned.1.call-start = ((), (), s32[]{:S(2)}) async-start(), calls=%async_computation.16 | async-start | bytes 3342336 | tf_op jit(solution)/shard_map/all_gather | solution.py:14
  8.8 70.6 %copy-start.114 = (s32[4,1]{0,1:T(1,128)}, s32[4,1]{0,1:T(1,128)S(1)}, u32[]{:S(2)}) copy-start(s32[4,1]{0,1:T(1,128)S(1)} %reduce-window.4) | copy-start | bytes 52
  8.8 51.4 %copy-start.95 = (f32[768]{0:T(1024)S(1)}, f32[768]{0:T(1024)}, u32[]{:S(2)}) copy-start(f32[768]{0:T(1024)} %param.26) | copy-start | bytes 9220
  8.8 51.4 %copy-start.111 = (f32[768]{0:T(1024)S(1)}, f32[768]{0:T(1024)}, u32[]{:S(2)}) copy-start(f32[768]{0:T(1024)} %param.27) | copy-start | bytes 9220
  8.8 51.4 %copy-start.119 = (f32[3,384]{1,0:T(4,128)S(1)}, f32[3,384]{1,0:T(4,128)}, u32[]{:S(2)}) copy-start(f32[3,384]{1,0:T(4,128)} %param.29) | copy-start | bytes 13828
  10.5 67.7 %copy-start.79 = (s32[512]{0:T(512)}, s32[512]{0:T(512)S(1)}, u32[]{:S(2)}) copy-start(s32[512]{0:T(512)S(1)} %select_select_fusion) | copy-start | bytes 6148
  11.1 57.6 %copy-start.92 = (f32[512]{0:T(512)}, f32[512]{0:T(512)S(1)}, u32[]{:S(2)}) copy-start(f32[512]{0:T(512)S(1)} %broadcast_multiply_fusion.2) | copy-start | bytes 6148
  11.5 57.3 %copy-start.99 = (f32[512]{0:T(512)}, f32[512]{0:T(512)S(1)}, u32[]{:S(2)}) copy-start(f32[512]{0:T(512)S(1)} %fusion.133) | copy-start | bytes 6148
  13.2 150.8 %copy-start.75 = (f32[512]{0:T(512)}, f32[512]{0:T(512)S(1)}, u32[]{:S(2)}) copy-start(f32[512]{0:T(512)S(1)} %get-tuple-element.642) | copy-start | bytes 6148
  72.0 429.7 %copy-start.58 = (f32[512,6]{0,1:T(8,128)}, f32[512,6]{0,1:T(8,128)S(1)}, u32[]{:S(2)}) copy-start(f32[512,6]{0,1:T(8,128)S(1)} %get-tuple-element.645) | copy-start | bytes 36868
  74.1 51.5 %copy-start.24 = (f32[512,6,64]{0,2,1:T(8,128)}, f32[512,6,64]{0,2,1:T(8,128)S(1)}, u32[]{:S(2)}) copy-start(f32[512,6,64]{0,2,1:T(8,128)S(1)} %get-tuple-element.656) | copy-start | bytes 2359300
  74.1 51.5 %copy-start.26 = (f32[512,6,64]{0,2,1:T(8,128)}, f32[512,6,64]{0,2,1:T(8,128)S(1)}, u32[]{:S(2)}) copy-start(f32[512,6,64]{0,2,1:T(8,128)S(1)} %get-tuple-element.657) | copy-start | bytes 2359300
  74.2 6.1 copy-start.123
  76.8 220.4 %all-gather.15.cloned.1.call-start = ((), (), s32[]{:S(2)}) async-start(), calls=%async_computation.7 | async-start | bytes 1253376 | tf_op jit(solution)/shard_map/all_gather | solution.py:156
  77.6 271.8 %all-gather.19.cloned.1.call-start = ((), (), s32[]{:S(2)}) async-start(), calls=%async_computation.10 | async-start | bytes 5013504 | tf_op jit(solution)/shard_map/all_gather | solution.py:158
  78.1 282.6 %all-reduce.9.cloned.1.call-start = ((), (), s32[]{:S(2)}) async-start(), calls=%async_computation.8 | async-start | bytes 3145728 | tf_op jit(solution)/shard_map/psum | solution.py:182
  129.2 33.3 %copy-start.32 = (f32[512,6,64]{0,2,1:T(8,128)}, f32[512,6,64]{0,2,1:T(8,128)S(1)}, u32[]{:S(2)}) copy-start(f32[512,6,64]{0,2,1:T(8,128)S(1)} %get-tuple-element.650) | copy-start | bytes 2359300
  129.2 33.3 %copy-start.63 = (f32[512,6]{0,1:T(8,128)}, f32[512,6]{0,1:T(8,128)S(1)}, u32[]{:S(2)}) copy-start(f32[512,6]{0,1:T(8,128)S(1)} %get-tuple-element.649) | copy-start | bytes 36868
  130.5 32.0 %copy-start.34 = (f32[512,6,64]{0,2,1:T(8,128)}, f32[512,6,64]{0,2,1:T(8,128)S(1)}, u32[]{:S(2)}) copy-start(f32[512,6,64]{0,2,1:T(8,128)S(1)} %get-tuple-element.652) | copy-start | bytes 2359300
  130.5 32.0 %copy-start.66 = (f32[512,6]{0,1:T(8,128)}, f32[512,6]{0,1:T(8,128)S(1)}, u32[]{:S(2)}) copy-start(f32[512,6]{0,1:T(8,128)S(1)} %get-tuple-element.651) | copy-start | bytes 36868
  162.6 126.7 %copy-start.2 = (f32[512,6,64]{0,2,1:T(8,128)}, f32[512,6,64]{0,2,1:T(8,128)S(1)}, u32[]{:S(2)}) copy-start(f32[512,6,64]{0,2,1:T(8,128)S(1)} %get-tuple-element.658) | copy-start | bytes 2359300
  162.6 126.7 %copy-start.5 = (f32[512,6,64]{0,2,1:T(8,128)}, f32[512,6,64]{0,2,1:T(8,128)S(1)}, u32[]{:S(2)}) copy-start(f32[512,6,64]{0,2,1:T(8,128)S(1)} %get-tuple-element.659) | copy-start | bytes 2359300
  297.2 6.6 copy-start.22
  303.8 106.3 %all-gather.17.cloned.1.call-start = ((), (), s32[]{:S(2)}) async-start(), calls=%async_computation.9 | async-start | bytes 5013504 | tf_op jit(solution)/shard_map/all_gather | solution.py:157
  304.4 5.6 copy-start.120
  304.4 39.4 %all-to-all-start.1 = ((f32[8,64,768]{2,1,0:T(8,128)}), f32[8,64,768]{2,1,0:T(8,128)S(1)}, u32[]{:S(2)}, u32[]{:S(2)}) async-start(f32[8,64,768]{2,1,0:T(8,128)} %bitcast.190), calls=%async_computation.1 | async-start | bytes 3145728 | tf_op jit(solution)/shard_map/all_to_all | solution.py:204
  308.0 177.9 %all-reduce.11.cloned.1.call-start = ((), (), s32[]{:S(2)}) async-start(), calls=%async_computation.11 | async-start | bytes 3145728 | tf_op jit(solution)/shard_map/psum | solution.py:215
  309.3 180.0 %copy-start.97 = (f32[512]{0:T(512)}, f32[512]{0:T(512)S(1)}, u32[]{:S(2)}) copy-start(f32[512]{0:T(512)S(1)} %fusion.132) | copy-start | bytes 6148
  310.0 35.6 %copy-start.121 = (s32[8]{0:T(128)}, s32[8]{0:T(128)S(1)}, u32[]{:S(2)}) copy-start(s32[8]{0:T(128)S(1)} %get-tuple-element.629) | copy-start | bytes 100
  349.3 11.5 copy-start.38
  349.3 11.5 copy-start.103
  362.4 47.7 %copy-start.73 = (f32[768]{0:T(1024)S(1)}, f32[768]{0:T(1024)}, u32[]{:S(2)}) copy-start(f32[768]{0:T(1024)} %param.34) | copy-start | bytes 9220
  362.4 47.7 %copy-start.83 = (f32[768]{0:T(1024)S(1)}, f32[768]{0:T(1024)}, u32[]{:S(2)}) copy-start(f32[768]{0:T(1024)} %param.35) | copy-start | bytes 9220
  362.4 47.7 %copy-start.118 = (f32[1536]{0:T(1024)S(1)}, f32[1536]{0:T(1024)}, u32[]{:S(2)}) copy-start(f32[1536]{0:T(1024)} %param.37) | copy-start | bytes 18436
  362.5 126.2 %copy-start.81 = (f32[512]{0:T(512)}, f32[512]{0:T(512)S(1)}, u32[]{:S(2)}) copy-start(f32[512]{0:T(512)S(1)} %broadcast_multiply_fusion.1) | copy-start | bytes 6148
  362.8 125.9 %copy-start.90 = (f32[512]{0:T(512)}, f32[512]{0:T(512)S(1)}, u32[]{:S(2)}) copy-start(f32[512]{0:T(512)S(1)} %fusion.134) | copy-start | bytes 6148
  410.1 16.5 %copy-start.117 = (f32[768,1536]{1,0:T(8,128)S(1)}, f32[768,1536]{1,0:T(8,128)}, u32[]{:S(2)}) copy-start(f32[768,1536]{1,0:T(8,128)} %all-gather.17.cloned.1.call-done) | copy-start | bytes 14155780
  435.7 117.6 %all-gather.23.cloned.1.call-start = ((), (), s32[]{:S(2)}) async-start(), calls=%async_computation.17 | async-start | bytes 3342336 | tf_op jit(solution)/shard_map/all_gather | solution.py:14
  497.9 322.7 %all-reduce.15.cloned.1.call-start = ((), (), s32[]{:S(2)}) async-start(), calls=%async_computation.19 | async-start | bytes 6291456 | tf_op jit(solution)/shard_map/psum | solution.py:196
  503.5 12.7 %copy-start.4 = (f32[512,6,64]{0,2,1:T(8,128)S(1)}, f32[512,6,64]{0,2,1:T(8,128)}, u32[]{:S(2)}) copy-start(f32[512,6,64]{0,2,1:T(8,128)} %copy-done.2) | copy-start | bytes 2359300
  503.5 12.7 %copy-start.7 = (f32[512,6,64]{0,2,1:T(8,128)S(1)}, f32[512,6,64]{0,2,1:T(8,128)}, u32[]{:S(2)}) copy-start(f32[512,6,64]{0,2,1:T(8,128)} %copy-done.5) | copy-start | bytes 2359300
  671.0 7.3 copy-start.9
  671.0 7.4 copy-start.16
  683.5 5.3 copy-start.13
  697.4 5.3 copy-start.17
  737.9 5.6 copy-start.74
  737.9 5.6 copy-start.82
  737.9 5.6 copy-start.84
  737.9 5.6 copy-start.91
  737.9 194.5 %reduce-scatter.7.cloned.1.call-start = ((), (), s32[]{:S(2)}) async-start(), calls=%async_computation.13 | async-start | bytes 1253376 | tf_op jit(solution)/shard_map/reduce_scatter | solution.py:255
  743.4 227.8 %reduce-scatter.9.cloned.1.call-start = ((), (), s32[]{:S(2)}) async-start(), calls=%async_computation.14 | async-start | bytes 5013504 | tf_op jit(solution)/shard_map/reduce_scatter | solution.py:256
  755.6 294.7 %reduce-scatter.11.cloned.1.call-start = ((), (), s32[]{:S(2)}) async-start(), calls=%async_computation.15 | async-start | bytes 5013504 | tf_op jit(solution)/shard_map/reduce_scatter | solution.py:257
  767.8 377.9 %all-reduce.13.cloned.1.call-start = ((), (), s32[]{:S(2)}) async-start(), calls=%async_computation.18 | async-start | bytes 786432 | tf_op jit(solution)/shard_map/psum | solution.py:259
  772.4 444.8 %reduce-scatter.5.cloned.1.call-start = ((), (), s32[]{:S(2)}) async-start(), calls=%async_computation.12 | async-start | bytes 3760128 | tf_op jit(solution)/shard_map/reduce_scatter | solution.py:254
  782.8 37.8 %copy-start.98 = (f32[512]{0:T(512)S(1)}, f32[512]{0:T(512)}, u32[]{:S(2)}) copy-start(f32[512]{0:T(512)} %copy-done.97) | copy-start | bytes 6148
  782.8 37.8 %copy-start.104 = (f32[768]{0:T(1024)S(1)}, f32[768]{0:T(1024)}, u32[]{:S(2)}) copy-start(f32[768]{0:T(1024)} %param.33) | copy-start | bytes 9220
  782.8 37.8 %copy-start.113 = (f32[768]{0:T(1024)S(1)}, f32[768]{0:T(1024)}, u32[]{:S(2)}) copy-start(f32[768]{0:T(1024)} %param.39) | copy-start | bytes 9220
  828.1 5.4 copy-start.36
  828.1 5.4 copy-start.37
  828.1 102.2 %all-to-all-start = ((f32[8,64,768]{2,1,0:T(8,128)}), f32[8,64,768]{2,1,0:T(8,128)}, u32[]{:S(2)}, u32[]{:S(2)}) async-start(f32[8,64,768]{2,1,0:T(8,128)} %broadcast_select_fusion.1), calls=%async_computation | async-start | bytes 3145728 | tf_op jit(solution)/shard_map/all_to_all | solution.py:199
  837.0 90.5 %copy-start.102 = (f32[512]{0:T(512)S(1)}, f32[512]{0:T(512)}, u32[]{:S(2)}) copy-start(f32[512]{0:T(512)} %copy-done.101) | copy-start | bytes 6148
  837.0 90.5 %copy-start.49 = (f32[512,768]{1,0:T(8,128)S(1)}, f32[512,768]{1,0:T(8,128)}, u32[]{:S(2)}) copy-start(f32[512,768]{1,0:T(8,128)} %get-tuple-element.616) | copy-start | bytes 4718596
  (77 other events, 181.6 us)
Sparse Core Ops, SparseCore 0:
  10.4 49.8 all-gather.12
  76.9 44.2 all-gather.20
  123.5 36.9 all-gather.14
  162.7 51.7 all-gather.18
  304.0 50.9 all-reduce.8
  357.1 52.9 all-gather.16
  435.8 50.0 all-reduce.10
  498.0 45.7 all-gather.22
  738.0 82.5 all-reduce.14
  824.7 67.4 reduce-scatter.6
  896.6 74.5 reduce-scatter.8
  975.5 74.7 reduce-scatter.10
  1054.9 90.7 all-reduce.12
  1150.0 67.1 reduce-scatter.4
where the time goes:
time: 1240 us; the launch traced here: 1230 us
  waiting for transfers between devices  503 us (41%)
  blocking collectives  200 us (16%)
  matrix products  192 us (15%)
  other arithmetic  149 us (12%)
  local copies, waits for them, and re-layouts  136 us (11%)
  loops' own time  21.4 us (2%)
  between operations  17.7 us (1%)
    select_n x64, other arithmetic, lap(): return jax.tree.map(lambda a, b: jnp.where(reached, a, b), new, before)  103 us
    dynamic_slice x96, local copies, waits for them, and re-layouts, lap(): new = combine(before, jax.tree.map(lambda part: part[at], everything))  99.5 us
    psum x1, waiting for transfers between devices, body(): lax.psum((grad_ln1_gain, grad_ln1_shift, grad_qkv_bias, grad_feat_query,...  95.4 us
    psum x1, blocking collectives, body(): lax.psum((grad_ln1_gain, grad_ln1_shift, grad_qkv_bias, grad_feat_query,...  89.3 us
    reduce_scatter x1, waiting for transfers between devices, body(): lax.psum_scatter(grad_down_full, ('fsdp', 'context'), scatter_dimension=1...  79.1 us
    reduce_scatter x1, waiting for transfers between devices, body(): lax.psum_scatter(grad_qkv_full, ('fsdp', 'context'), scatter_dimension=0,...  71.5 us
    all_gather x2, blocking collectives, entering(): everything = jax.tree.map(lambda part: lax.all_gather(part, axis), x)  67.3 us
    psum x1, waiting for transfers between devices, body(): grad_normed2 = lax.psum(grad_normed2_part, 'tensor')  50 us
  transfers between devices with their start and end apart: 16, of which 9 were waited for; matrix products, arithmetic and copies ran while one was open for 20% of the time, Pallas kernels for 0%

commit v1 on v0

v1 whole, which is shorter than its diff:
```python
import jax
import jax.numpy as jnp
from jax import lax
from jax.sharding import PartitionSpec as P

HIGH = lax.Precision.HIGH
FULL = lax.Precision.HIGHEST
NORM_EPS = 1e-05
DATA = ("fsdp", "context")
GELU_SCALE = 0.7978845608028654
GELU_CUBE = 0.044715


def dot(a, b, over, batch=((), ()), precision=HIGH):
    return lax.dot_general(
        a, b, (over, batch), precision=precision, preferred_element_type=jnp.float32
    )


def swap_with(axis, bit):
    count = lax.axis_size(axis)
    return [(i, i ^ bit) for i in range(count)]


def tensor_sum(part):
    count = lax.axis_size("tensor")
    bit = 1
    while bit < count:
        part = part + lax.ppermute(part, "tensor", swap_with("tensor", bit))
        bit *= 2
    return part


def data_sum(part):
    for axis in DATA:
        count = lax.axis_size(axis)
        bit = 1
        while bit < count:
            part = part + lax.ppermute(part, axis, swap_with(axis, bit))
            bit *= 2
    return part


def gather_rows(shard):
    return lax.all_gather(shard, DATA, axis=0, tiled=True)


def scatter_rows(whole):
    return lax.psum_scatter(whole, DATA, scatter_dimension=0, tiled=True)


def chain(state, normer, joins):
    heads, feats, head_dim = state.shape
    count = joins.shape[0]
    packed = jnp.concatenate([jnp.swapaxes(state, 1, 2), normer[:, None, :]], axis=1)
    lines = heads * (head_dim + 1)
    share = -(-lines // (8 * count)) * 8
    packed = jnp.pad(packed.reshape(lines, feats), ((0, share * count - lines), (0, 0)))
    slices = lax.all_to_all(
        packed.reshape(count, share, feats), DATA, split_axis=0, concat_axis=0, tiled=True
    )
    joined = dot(joins, slices.reshape(count, share * feats), ((1,), (0,)), precision=FULL)
    back = lax.all_to_all(
        joined.reshape(count, share, feats), DATA, split_axis=0, concat_axis=0, tiled=True
    )
    back = back.reshape(share * count, feats)[:lines].reshape(heads, head_dim + 1, feats)
    return back[:, :head_dim], back[:, head_dim]


def row_stats(values):
    middle = jnp.mean(values, axis=-1, keepdims=True)
    centred = values - middle
    spread = jnp.mean(centred * centred, axis=-1, keepdims=True)
    scale = lax.rsqrt(spread + NORM_EPS)
    return centred * scale, scale


def norm_backward(grad, hat, scale, gain):
    scaled = grad * gain
    return (
        scaled
        - jnp.mean(scaled, axis=-1, keepdims=True)
        - hat * jnp.mean(scaled * hat, axis=-1, keepdims=True)
    ) * scale


def body(
    block_input,
    ln1_gain,
    ln1_shift,
    qkv_weight,
    qkv_bias,
    feat_query,
    feat_key,
    out_weight,
    out_bias,
    ln2_gain,
    ln2_shift,
    up_weight,
    up_bias,
    down_weight,
    down_bias,
    lengths,
    deal,
    cotangent,
):
    rows, width = block_input.shape
    heads, head_dim = (feat_query.shape[0], feat_query.shape[1])
    local = heads * head_dim
    hidden_units = up_weight.shape[1]
    count = lax.axis_size(DATA)
    me = lax.axis_index(DATA)
    ends = jnp.cumsum(lengths)
    used = ends[-1]
    places = me * rows + jnp.arange(rows, dtype=jnp.int32)

    def segment_of(at):
        return jnp.sum((ends[None, :] <= at[:, None]).astype(jnp.int32), axis=1)

    segment = segment_of(places)
    starts = jnp.arange(count, dtype=jnp.int32) * rows
    firsts = segment_of(starts)
    finals = segment_of(starts + (rows - 1))
    order = jnp.arange(count)
    joins = jnp.logical_and(
        order[None, :] < order[:, None], finals[None, :] == firsts[:, None]
    ).astype(jnp.float32)
    from_first = (segment == segment[0]).astype(jnp.float32)
    to_final = (segment == segment[-1]).astype(jnp.float32)
    valid = (places < used).astype(jnp.float32)[:, None]
    lower = jnp.arange(rows)[:, None] >= jnp.arange(rows)[None, :]
    allowed = jnp.logical_and(lower, segment[:, None] == segment[None, :])

    first_pack = jnp.concatenate([qkv_weight.reshape(-1, 3 * local), out_weight.T], axis=1)
    second_pack = jnp.concatenate([up_weight, down_weight.T], axis=1)
    first_full = gather_rows(first_pack)
    second_full = gather_rows(second_pack)
    qkv_full = first_full[:, : 3 * local]
    out_full = first_full[:, 3 * local :]
    up_full = second_full[:, :hidden_units]
    down_full = second_full[:, hidden_units:]

    slots = deal.shape[0]
    group_rows = rows // slots
    tensor = lax.axis_size("tensor")
    part_rows = group_rows // tensor
    part_start = lax.axis_index("tensor") * part_rows
    per_peer = slots // lax.axis_size("context")
    slot_of = deal // slots % lax.axis_size("context") * per_peer + deal % per_peer
    counting = jnp.arange(slots, dtype=jnp.int32)
    source_of = jnp.sum(
        jnp.where(slot_of[None, :] == counting[:, None], counting[None, :], 0), axis=1
    )
    inbound = lax.all_to_all(
        cotangent.reshape(slots, group_rows, width),
        "context",
        split_axis=0,
        concat_axis=0,
        tiled=True,
    )

    hat1, scale1 = row_stats(block_input)
    normed1 = hat1 * ln1_gain + ln1_shift
    qkv = dot(normed1, qkv_full, ((1,), (0,))) + qkv_bias.reshape(1, 3 * local)
    split = qkv.reshape(rows, 3, heads, head_dim).transpose(1, 2, 0, 3)
    queries, keys, values = (split[0], split[1], split[2])

    def features(part, weight):
        logits = dot(part, weight, ((2,), (1,)), ((0,), (0,)))
        return jax.nn.softmax(logits, axis=-1), jax.nn.softmax(-logits, axis=-1)

    query_p, query_m = features(queries, feat_query)
    key_p, key_m = features(keys, feat_key)
    phi_q = jnp.concatenate([query_p, query_m], axis=-1)
    phi_k = jnp.concatenate([key_p, key_m], axis=-1)
    tail_k = phi_k * to_final[None, :, None]
    heads_b = ((0,), (0,))
    state_tail = dot(tail_k, values, ((1,), (1,)), heads_b)
    state_in, norm_in = chain(state_tail, jnp.sum(tail_k, axis=1), joins)
    scores = jnp.where(allowed[None], dot(phi_q, phi_k, ((2,), (2,)), heads_b), 0.0)
    head_q = phi_q * from_first[None, :, None]
    numer = dot(scores, values, ((2,), (1,)), heads_b) + dot(
        head_q, state_in, ((2,), (2,)), heads_b
    )
    denom = jnp.sum(scores, axis=2) + jnp.sum(head_q * norm_in[:, None, :], axis=2)
    attended = numer / denom[:, :, None]
    flat = attended.transpose(1, 0, 2).reshape(rows, local)
    attn = tensor_sum(dot(flat, out_full, ((1,), (1,)))) + out_bias
    hidden = block_input + attn

    hat2, scale2 = row_stats(hidden)
    normed2 = hat2 * ln2_gain + ln2_shift
    pre = dot(normed2, up_full, ((1,), (0,))) + up_bias
    bent = jnp.tanh(GELU_SCALE * (pre + GELU_CUBE * pre * pre * pre))
    active = 0.5 * pre * (1.0 + bent)
    slope = 0.5 * (1.0 + bent) + 0.5 * pre * (1.0 - bent * bent) * GELU_SCALE * (
        1.0 + 3.0 * GELU_CUBE * pre * pre
    )
    mlp_terms = dot(active, down_full, ((1,), (1,)))

    def own_part(array):
        return lax.dynamic_slice_in_dim(
            array.reshape(slots, group_rows, width), part_start, part_rows, 1
        )

    if tensor == 2:
        other = lax.dynamic_slice_in_dim(
            mlp_terms.reshape(slots, group_rows, width), part_rows - part_start, part_rows, 1
        )
        mlp_own = own_part(mlp_terms) + lax.ppermute(other, "tensor", [(0, 1), (1, 0)])
    else:
        mlp_own = own_part(tensor_sum(mlp_terms))
    mlp_own = mlp_own + down_bias
    attn_own = own_part(attn)
    result = own_part(hidden) + mlp_own
    outbound = jnp.take(result, source_of, axis=0)
    dealt_output = lax.all_to_all(outbound, "context", split_axis=0, concat_axis=0, tiled=True)
    weight_own = own_part(jnp.broadcast_to(valid, (rows, width)))[:, :, :1]
    squares = jnp.stack(
        [
            jnp.sum(weight_own * result * result),
            jnp.sum(weight_own * attn_own * attn_own),
            jnp.sum(weight_own * mlp_own * mlp_own),
        ]
    )

    grad_y = jnp.take(inbound, slot_of, axis=0).reshape(rows, width) * valid
    grad_pre = dot(grad_y, down_full, ((1,), (0,))) * slope
    grad_normed2 = tensor_sum(dot(grad_pre, up_full, ((1,), (1,))))
    second_grad = jnp.concatenate(
        [dot(normed2, grad_pre, ((0,), (0,))), dot(grad_y, active, ((0,), (0,)))], axis=1
    )
    second_own = scatter_rows(second_grad)
    grad_hidden = grad_y + norm_backward(grad_normed2, hat2, scale2, ln2_gain)

    out_grad = dot(grad_hidden, flat, ((0,), (0,)))
    grad_flat = dot(grad_hidden, out_full, ((1,), (0,)))
    grad_attended = grad_flat.reshape(rows, heads, head_dim).transpose(1, 0, 2)
    grad_numer = grad_attended / denom[:, :, None]
    grad_denom = -jnp.sum(grad_attended * attended, axis=2) / denom
    state_grad_in = dot(head_q, grad_numer, ((1,), (1,)), heads_b)
    norm_grad_in = jnp.sum(head_q * grad_denom[:, :, None], axis=1)
    state_grad, norm_grad = chain(state_grad_in, norm_grad_in, joins.T)
    pulls = jnp.where(
        allowed[None],
        dot(grad_numer, values, ((2,), (2,)), heads_b) + grad_denom[:, :, None],
        0.0,
    )
    grad_phi_q = dot(pulls, phi_k, ((2,), (1,)), heads_b) + from_first[None, :, None] * (
        dot(grad_numer, state_in, ((2,), (1,)), heads_b)
        + grad_denom[:, :, None] * norm_in[:, None, :]
    )
    grad_phi_k = dot(pulls, phi_q, ((1,), (1,)), heads_b) + to_final[None, :, None] * (
        dot(values, state_grad, ((2,), (1,)), heads_b) + norm_grad[:, None, :]
    )
    grad_values = dot(scores, grad_numer, ((1,), (1,)), heads_b) + dot(
        tail_k, state_grad, ((2,), (2,)), heads_b
    )

    def features_back(part, weight, plus, minus, grad):
        up, down = (grad[:, :, :head_dim], grad[:, :, head_dim:])
        grad_logits = plus * (up - jnp.sum(up * plus, axis=-1, keepdims=True)) - minus * (
            down - jnp.sum(down * minus, axis=-1, keepdims=True)
        )
        return (
            dot(grad_logits, weight, ((2,), (2,)), heads_b),
            dot(part, grad_logits, ((1,), (1,)), heads_b),
        )

    grad_queries, grad_feat_query = features_back(queries, feat_query, query_p, query_m, grad_phi_q)
    grad_keys, grad_feat_key = features_back(keys, feat_key, key_p, key_m, grad_phi_k)
    grad_qkv = (
        jnp.stack([grad_queries, grad_keys, grad_values])
        .transpose(2, 0, 1, 3)
        .reshape(rows, 3 * local)
    )
    grad_normed1_part = dot(grad_qkv, qkv_full, ((1,), (1,)))
    first_grad = jnp.concatenate([dot(normed1, grad_qkv, ((0,), (0,))), out_grad], axis=1)
    first_own = scatter_rows(first_grad)
    grad_normed1 = tensor_sum(grad_normed1_part)
    grad_input = grad_hidden + norm_backward(grad_normed1, hat1, scale1, ln1_gain)

    crossing = tensor_sum(
        jnp.concatenate(
            [
                jnp.sum(grad_normed1_part * hat1, axis=0),
                jnp.sum(grad_normed1_part, axis=0),
                jnp.pad(squares, (0, 125)),
            ]
        )
    )
    small = [
        grad_feat_query.reshape(-1),
        grad_feat_key.reshape(-1),
        jnp.sum(grad_qkv, axis=0),
        jnp.sum(grad_hidden, axis=0),
        jnp.sum(grad_normed2 * hat2, axis=0),
        jnp.sum(grad_normed2, axis=0),
        jnp.sum(grad_pre, axis=0),
        jnp.sum(grad_y, axis=0),
        crossing,
    ]
    joined = jnp.concatenate(small)
    joined = jnp.pad(joined, (0, -joined.shape[0] % 1024))
    total = data_sum(joined.reshape(-1, 128)).reshape(-1)
    pieces = []
    at = 0
    for part in small:
        pieces.append(total[at : at + part.shape[0]])
        at += part.shape[0]
    last = pieces[8]
    rms = jnp.sqrt(last[2 * width : 2 * width + 3] / (used.astype(jnp.float32) * width))
    return (
        dealt_output,
        rms,
        grad_input,
        last[:width],
        last[width : 2 * width],
        first_own[:, : 3 * local].reshape(-1, 3, local),
        pieces[2].reshape(3, local),
        pieces[0].reshape(feat_query.shape),
        pieces[1].reshape(feat_key.shape),
        first_own[:, 3 * local :].T,
        pieces[3],
        pieces[4],
        pieces[5],
        second_own[:, :hidden_units],
        pieces[6],
        second_own[:, hidden_units:].T,
        pieces[7],
    )


def solution(mesh):
    in_specs = (
        P(("fsdp", "context"), None),
        P(),
        P(),
        P(("fsdp", "context"), None, "tensor"),
        P(None, "tensor"),
        P("tensor", None, None),
        P("tensor", None, None),
        P("tensor", ("fsdp", "context")),
        P(),
        P(),
        P(),
        P(("fsdp", "context"), "tensor"),
        P("tensor"),
        P("tensor", ("fsdp", "context")),
        P(),
        P(),
        P(("fsdp", "context")),
        P(("fsdp", "context"), None),
    )
    out_specs = (
        P(("fsdp", "context"), "tensor", None),
        P(),
        P(("fsdp", "context"), None),
        P(),
        P(),
        P(("fsdp", "context"), None, "tensor"),
        P(None, "tensor"),
        P("tensor", None, None),
        P("tensor", None, None),
        P("tensor", ("fsdp", "context")),
        P(),
        P(),
        P(),
        P(("fsdp", "context"), "tensor"),
        P("tensor"),
        P("tensor", ("fsdp", "context")),
        P(),
    )
    return jax.shard_map(body, mesh=mesh, in_specs=in_specs, out_specs=out_specs, check_vma=False)
```

time: 1240 us -> 564 us (0.45)
  waiting for transfers between devices: 503 us -> 256 us
  blocking collectives: 200 us -> 0 us
  other arithmetic: 149 us -> 58.6 us
  local copies, waits for them, and re-layouts: 136 us -> 50.7 us
  matrix products: 192 us -> 132 us
  starting transfers between devices: 9.22 us -> 40.7 us
  loops' own time: 21.4 us -> 0 us
    psum x4 -> x0, waiting for transfers between devices: 182 us -> none  [the longest x1 95.4 us: body(): lax.psum((grad_ln1_gain, grad_ln1_shift, grad_qkv_bias, grad_feat_query,...]
    reduce_scatter x4 -> x2, waiting for transfers between devices: 189 us -> 27.6 us  [scatter_rows(): return lax.psum_scatter(whole, DATA, scatter_dimension=0, tiled=True)]
    ppermute x0 -> x9, waiting for transfers between devices: none -> 122 us  [the longest x4 59.8 us: tensor_sum(): part = part + lax.ppermute(part, 'tensor', swap_with('tensor', bit))]
    select_n x69 -> x3, other arithmetic: 104 us -> 1.02 us  [the longest x2 1.01 us: body(): outbound = jnp.take(result, source_of, axis=0)]
    dynamic_slice x97 -> x2, local copies, waits for them, and re-layouts: 102 us -> 1.03 us  [the longest x1 0.95 us: body(): lax.dynamic_slice_in_dim(mlp_terms.reshape(slots, group_rows, width), par...]
    psum x1 -> x0, blocking collectives: 89.3 us -> none  [body(): lax.psum((grad_ln1_gain, grad_ln1_shift, grad_qkv_bias, grad_feat_query,...]
    all_gather x2 -> x0, blocking collectives: 67.3 us -> none  [entering(): everything = jax.tree.map(lambda part: lax.all_gather(part, axis), x)]
    dot_general x36 -> x32, matrix products: 192 us -> 132 us  [dot(): lax.dot_general(a, b, (over, batch), precision=precision, preferred_eleme...]
  transfers between devices with their start and end apart: 16 -> 19, of which waited for: 9 -> 14; matrix products, arithmetic and copies ran while one was open for 20% -> 30% of each run, Pallas kernels for 0% -> 0%
where the time goes in v1:
time: 564 us; the launch traced here: 554 us
  waiting for transfers between devices  256 us (45%)
  matrix products  132 us (23%)
  other arithmetic  58.6 us (10%)
  local copies, waits for them, and re-layouts  50.7 us (9%)
  starting transfers between devices  40.7 us (7%)
  between operations  16 us (3%)
    dot_general x32, matrix products, dot(): lax.dot_general(a, b, (over, batch), precision=precision, preferred_eleme...  132 us
    ppermute x4, waiting for transfers between devices, tensor_sum(): part = part + lax.ppermute(part, 'tensor', swap_with('tensor', bit))  59.8 us
    all_gather x2, waiting for transfers between devices, gather_rows(): return lax.all_gather(shard, DATA, axis=0, tiled=True)  50.3 us
    ppermute x4, waiting for transfers between devices, data_sum(): part = part + lax.ppermute(part, axis, swap_with(axis, bit))  46.5 us
    all_to_all x1, waiting for transfers between devices, body(): lax.all_to_all(cotangent.reshape(slots, group_rows, width), 'context', sp...  33.4 us
    reduce_scatter x2, waiting for transfers between devices, scatter_rows(): return lax.psum_scatter(whole, DATA, scatter_dimension=0, tiled=True)  27.6 us
    unnamed x199, local copies, waits for them, and re-layouts  20.5 us
    ppermute x1, waiting for transfers between devices, body(): lax.ppermute(other, 'tensor', [(0, 1), (1, 0)])  15.7 us
  transfers between devices with their start and end apart: 19, of which 14 were waited for; matrix products, arithmetic and copies ran while one was open for 30% of the time, Pallas kernels for 0%

profile of v1, /device:TPU:0, one launch (start us, length us, event | category | flops | bytes accessed | tf_op | source)
XLA Modules:
  0.0 553.9 jit_solution(12646662166950561617)
XLA Ops:
  8.4 1.6 pad_maximum_fusion.10
  10.1 1.9 pad_maximum_fusion.5
  16.3 50.3 %all-gather.3.cloned.1.call-done = f32[768,1536]{1,0:T(8,128)} async-done(((f32[48,1536]{1,0:T(8,128)}), f32[768,1536]{1,0:T(8,128)}) %all-gather.3.cloned.1.call-update) | async-done | bytes 4718608 | tf_op jit(solution)/shard_map/all_gather | solution.py:45
  66.6 6.9 %convolution_add_fusion = f32[512,1152]{1,0:T(8,128)} fusion(f32[768,1536]{1,0:T(8,128)} %all-gather.3.cloned.1.call-done, f32[1152]{0:T(1024)S(1)} %add.263, f32[512,768]{1,0:T(8,128)S(1)} %copy-done.2, f32[768]{0:T(1024)S(1)} %copy-done.78, f32[768]{0:T(1024)S(1)} %copy-done.65, f32[512]{0:T(512)S(1)} %add_rsqrt_fusion.1, f32[512]{0:T(512)S(1)} %broadcast_multiply_fusion.5), kind=kOutput, calls=%fused_computation.26 | convolution fusion | flops 2720071680 | bytes 7485952 | tf_op jit(solution)/shard_map/dot_general | solution.py:15
  73.5 3.3 copy.97
  76.8 1.7 fusion.98
  81.3 2.1 fusion.52
  85.8 4.2 all-to-all-start
  90.0 1.7 fusion.96
  93.8 11.4 %all-to-all-done = f32[16,32,128]{2,1,0:T(8,128)} async-done(((f32[16,32,128]{2,1,0:T(8,128)}), f32[16,32,128]{2,1,0:T(8,128)}, u32[]{:S(2)}, u32[]{:S(2)}) %all-to-all-start) | async-done | bytes 262176 | tf_op jit(solution)/shard_map/all_to_all | solution.py:59
  107.4 4.2 all-to-all-start.1
  111.6 1.6 broadcast_divide_fusion.3
  114.4 5.6 %select_reduce_fusion = (f32[6,512]{1,0:T(8,128)}, f32[6,512,512]{1,2,0:T(8,128)}) fusion(pred[512,512]{0,1:T(8,128)(4,1)S(1)} %copy-done.21, f32[6,512,64]{1,2,0:T(8,128)S(1)} %get-tuple-element.140, f32[6,512,64]{1,2,0:T(8,128)S(1)} %get-tuple-element.141, f32[6,512,64]{1,2,0:T(8,128)S(1)} %get-tuple-element.142, f32[6,512,64]{1,2,0:T(8,128)S(1)} %get-tuple-element.143), kind=kOutput, calls=%fused_computation.12 | convolution fusion | flops 1211888640 | bytes 9711616 | tf_op jit(solution)/shard_map/dot_general | solution.py:15
  120.0 9.6 %all-to-all-done.1 = f32[16,32,128]{2,1,0:T(8,128)} async-done(((f32[16,32,128]{2,1,0:T(8,128)}), f32[16,32,128]{2,1,0:T(8,128)}, u32[]{:S(2)}, u32[]{:S(2)}) %all-to-all-start.1) | async-done | bytes 262176 | tf_op jit(solution)/shard_map/all_to_all | solution.py:63
  129.6 4.6 all-to-all-start.3
  134.2 6.2 %fusion.8 = f32[6,512,64]{1,2,0:T(8,128)} fusion(f32[6,512,512]{1,2,0:T(8,128)} %get-tuple-element.135, pred[512,512]{0,1:T(8,128)(4,1)} %fusion.71, f32[3,6,512,64]{2,3,1,0:T(8,128)} %bitcast.157), kind=kOutput, calls=%fused_computation.13 | convolution fusion | flops 605552640 | bytes 8126464 | tf_op jit(solution)/shard_map/dot_general | solution.py:15
  144.6 2.7 bitcast_divide_fusion
  147.4 4.9 fusion.69
  155.2 33.4 %all-to-all-done.3 = f32[8,64,768]{2,1,0:T(8,128)} async-done(((f32[8,64,768]{2,1,0:T(8,128)}), f32[8,64,768]{2,1,0:T(8,128)}, u32[]{:S(2)}, u32[]{:S(2)}) %all-to-all-start.3) | async-done | bytes 1572896 | tf_op jit(solution)/shard_map/all_to_all | solution.py:154
  188.6 3.2 gather_fusion.1
  191.8 2.8 fusion.42
  194.6 3.3 fusion.149
  199.4 7.3 %fusion.24 = f32[512,1536]{1,0:T(8,128)S(1)} fusion(f32[768,3072]{1,0:T(8,128)} %all-gather.5.cloned.1.call-done, f32[1536]{0:T(1024)S(1)} %copy-done.85, f32[512,768]{1,0:T(8,128)} %copy-done.3, f32[768]{0:T(1024)S(1)} %copy-done.75, f32[768]{0:T(1024)S(1)} %copy-done.53, f32[512]{0:T(512)S(1)} %add_rsqrt_fusion, f32[512]{0:T(512)S(1)} %broadcast_multiply_fusion.4), kind=kOutput, calls=%fused_computation.31 | convolution fusion | flops 3626237952 | bytes 9453568 | tf_op jit(solution)/shard_map/dot_general | solution.py:15
  206.8 8.4 %fusion.156 = (f32[1536]{0:T(1024)}, f32[512,1536]{1,0:T(8,128)S(1)}) fusion(f32[512,1536]{1,0:T(8,128)S(1)} %fusion.24, f32[512,768]{1,0:T(8,128)} %fusion.42, f32[768,3072]{1,0:T(8,128)S(1)} %copy-done.39), kind=kOutput, calls=%fused_computation.283 | convolution fusion | flops 3638819328 | bytes 12589056 | tf_op jit(solution)/shard_map/dot_general | solution.py:15
  215.2 4.0 fusion.14
  220.7 34.6 %collective-permute-done.2 = f32[512,768]{1,0:T(8,128)S(1)} collective-permute-done((f32[512,768]{1,0:T(8,128)S(1)}, f32[512,768]{1,0:T(8,128)S(1)}, u32[]{:S(2)}, u32[]{:S(2)}) %collective-permute-start.2) | collective-permute-done | bytes 1572896 | tf_op jit(solution)/shard_map/ppermute | solution.py:29
  258.3 3.7 fusion.157
  262.1 2.5 fusion.67
  265.6 5.9 %fusion.101 = f32[6,512,512]{1,2,0:T(8,128)} fusion(f32[3,6,512,64]{2,3,1,0:T(8,128)} %bitcast.158, f32[6,512,64]{1,2,0:T(8,128)S(1)} %bitcast.165, f32[6,512]{1,0:T(8,128)S(1)} %add.269), kind=kOutput, calls=%fused_computation.151 | convolution fusion | flops 604176384 | bytes 7876608 | tf_op jit(solution)/shard_map/dot_general | solution.py:15
  274.6 4.4 all-to-all-start.4
  279.1 5.4 fusion.5
  288.8 4.2 fusion.6
  295.2 6.1 %all-to-all-start.5 = ((f32[16,32,128]{2,1,0:T(8,128)}), f32[16,32,128]{2,1,0:T(8,128)}, u32[]{:S(2)}, u32[]{:S(2)}) async-start(f32[16,32,128]{2,1,0:T(8,128)} %copy.113), calls=%async_computation.5 | async-start | bytes 524288 | tf_op jit(solution)/shard_map/all_to_all | solution.py:63
  301.7 8.0 %fusion.4 = f32[6,512,128]{1,2,0:T(8,128)} fusion(f32[6,512,512]{1,2,0:T(8,128)} %fusion.101, f32[6,512]{1,0:T(8,128)S(1)} %copy-done.50, pred[512,512]{0,1:T(8,128)(4,1)} %fusion.71, f32[6,512,64]{1,2,0:T(8,128)} %copy-done.6, f32[6,512,64]{1,2,0:T(8,128)} %copy-done.10), kind=kOutput, calls=%fused_computation.8 | convolution fusion | flops 1211498496 | bytes 9711616 | tf_op jit(solution)/shard_map/dot_general | solution.py:15
  313.5 1.9 fusion.61
  315.4 2.3 multiply_add_fusion.2
  322.9 6.9 %fusion.48 = f32[768,1152]{1,0:T(8,128)S(1)} fusion(f32[512,1152]{0,1:T(8,128)S(1)} %bitcast.162, f32[512,768]{1,0:T(8,128)S(1)} %copy-done.2, f32[768]{0:T(1024)S(1)} %copy-done.79, f32[768]{0:T(1024)S(1)} %copy-done.66, f32[512]{0:T(512)S(1)} %copy-done.58, f32[512]{0:T(512)S(1)} %broadcast_multiply_fusion.5), kind=kOutput, calls=%fused_computation.78 | convolution fusion | flops 2719481856 | bytes 7481344 | tf_op jit(solution)/shard_map/dot_general | solution.py:15
  329.8 2.9 pad_maximum_fusion.1
  334.1 6.4 %fusion.49 = f32[768,1536]{1,0:T(8,128)S(1)} fusion(f32[512,1536]{1,0:T(8,128)} %copy-done.18, f32[512,768]{1,0:T(8,128)S(1)} %copy-done.5, f32[768]{0:T(1024)S(1)} %copy-done.76, f32[768]{0:T(1024)S(1)} %copy-done.54, f32[512]{0:T(512)S(1)} %copy-done.56, f32[512]{0:T(512)S(1)} %broadcast_multiply_fusion.4), kind=kOutput, calls=%fused_computation.79 | convolution fusion | flops 3625451520 | bytes 9447424 | tf_op jit(solution)/shard_map/dot_general | solution.py:15
  340.5 6.2 %fusion.43 = f32[768,1536]{1,0:T(8,128)} fusion(f32[512,768]{1,0:T(8,128)S(1)} %copy-done.41, f32[512,1536]{1,0:T(8,128)S(1)} %copy-done.91), kind=kOutput, calls=%fused_computation.73 | convolution fusion | flops 3630170112 | bytes 9437184 | tf_op jit(solution)/shard_map/dot_general | solution.py:15
  346.7 7.3 %pad_maximum_fusion = f32[768,3072]{1,0:T(8,128)} fusion(f32[768,1536]{1,0:T(8,128)} %fusion.43, f32[768,1536]{1,0:T(8,128)S(1)} %fusion.49), kind=kLoop, calls=%fused_computation.6 | loop fusion | flops 2359296 | bytes 18874368 | tf_op jit(solution)/shard_map/concatenate | solution.py:230
  354.8 7.9 %fusion.12 = f32[512,768]{1,0:T(8,128)S(1)} fusion(f32[768,3072]{1,0:T(8,128)} %all-gather.5.cloned.1.call-done, f32[512,1536]{1,0:T(8,128)} %copy-done.90), kind=kOutput, calls=%fused_computation.20 | convolution fusion | flops 3630170112 | bytes 9437184 | tf_op jit(solution)/shard_map/dot_general | solution.py:15
  367.2 1.6 multiply_reduce_fusion.2
  368.8 15.7 %collective-permute-done.1 = f32[8,32,768]{2,1,0:T(8,128)} collective-permute-done((f32[8,32,768]{2,1,0:T(8,128)}, f32[8,32,768]{2,1,0:T(8,128)}, u32[]{:S(2)}, u32[]{:S(2)}) %collective-permute-start.1) | collective-permute-done | bytes 786464 | tf_op jit(solution)/shard_map/ppermute | solution.py:210
  384.5 3.1 fusion.72
  387.6 1.7 gather_fusion
  390.4 4.4 all-to-all-start.2
  394.8 2.0 select_maximum_fusion
  396.9 1.6 fusion.95
  398.6 9.7 %fusion.21 = f32[512,768]{1,0:T(8,128)} fusion(f32[512,1152]{0,1:T(8,128)} %bitcast.163, f32[768,1536]{1,0:T(8,128)} %all-gather.3.cloned.1.call-done), kind=kOutput, calls=%fused_computation.28 | convolution fusion | flops 2717908992 | bytes 7471104 | tf_op jit(solution)/shard_map/dot_general | solution.py:15
  410.4 1.7 fusion.97
  420.8 23.1 %collective-permute-done.8 = f32[512,768]{1,0:T(8,128)} collective-permute-done((f32[512,768]{1,0:T(8,128)}, f32[512,768]{1,0:T(8,128)}, u32[]{:S(2)}, u32[]{:S(2)}) %collective-permute-start.8) | collective-permute-done | bytes 1572896 | tf_op jit(solution)/shard_map/ppermute | solution.py:29
  444.0 3.8 multiply_reduce_fusion
  447.7 1.6 collective-permute-start.3
  449.4 2.1 collective-permute-done.3
  453.8 1.8 collective-permute-start.5
  456.3 10.7 %collective-permute-done.5 = f32[448,128]{1,0:T(8,128)} collective-permute-done((f32[448,128]{1,0:T(8,128)}, f32[448,128]{1,0:T(8,128)}, u32[]{:S(2)}, u32[]{:S(2)}) %collective-permute-start.5) | collective-permute-done | bytes 229408 | tf_op jit(solution)/shard_map/ppermute | solution.py:39
  468.2 1.9 collective-permute-start.6
  470.1 21.5 %collective-permute-done.6 = f32[448,128]{1,0:T(8,128)S(1)} collective-permute-done((f32[448,128]{1,0:T(8,128)S(1)}, f32[448,128]{1,0:T(8,128)S(1)}, u32[]{:S(2)}, u32[]{:S(2)}) %collective-permute-start.6) | collective-permute-done | bytes 229408 | tf_op jit(solution)/shard_map/ppermute | solution.py:39
  492.5 3.0 multiply_add_fusion.1
  495.5 12.8 %collective-permute-done.7 = f32[448,128]{1,0:T(8,128)S(1)} collective-permute-done((f32[448,128]{1,0:T(8,128)S(1)}, f32[448,128]{1,0:T(8,128)S(1)}, u32[]{:S(2)}, u32[]{:S(2)}) %collective-permute-start.7) | collective-permute-done | bytes 229408 | tf_op jit(solution)/shard_map/ppermute | solution.py:39
  515.5 27.6 %reduce-scatter.5.cloned.1.call-done = f32[48,3072]{1,0:T(8,128)} async-done(((f32[768,3072]{1,0:T(8,128)}), f32[48,3072]{1,0:T(8,128)}) %reduce-scatter.5.cloned.1.call-update) | async-done | bytes 589840 | tf_op jit(solution)/shard_map/reduce_scatter | solution.py:49
  543.1 1.9 slice_bitcast_fusion.11
  545.0 2.1 copy.171
  (319 shorter events, 79.0 us)
Async XLA Ops:
  7.2 82.8 %copy-start = (f32[6,64,64]{2,1,0:T(8,128)S(1)}, f32[6,64,64]{2,1,0:T(8,128)}, u32[]{:S(2)}) copy-start(f32[6,64,64]{2,1,0:T(8,128)} %param.23) | copy-start | bytes 294916
  7.2 4.8 copy-start.70
  7.2 59.4 %all-gather.3.cloned.1.call-start = ((), (), s32[]{:S(2)}) async-start(), calls=%async_computation.8 | async-start | bytes 5013504 | tf_op jit(solution)/shard_map/all_gather | solution.py:45
  7.3 4.8 copy-start.86
  7.3 5.0 copy-start.2
  10.0 189.4 %all-gather.5.cloned.1.call-start = ((), (), s32[]{:S(2)}) async-start(), calls=%async_computation.9 | async-start | bytes 10027008 | tf_op jit(solution)/shard_map/all_gather | solution.py:45
  12.2 54.4 %copy-start.65 = (f32[768]{0:T(1024)S(1)}, f32[768]{0:T(1024)}, u32[]{:S(2)}) copy-start(f32[768]{0:T(1024)} %param.19) | copy-start | bytes 9220
  12.2 54.4 %copy-start.78 = (f32[768]{0:T(1024)S(1)}, f32[768]{0:T(1024)}, u32[]{:S(2)}) copy-start(f32[768]{0:T(1024)} %param.20) | copy-start | bytes 9220
  14.1 52.5 %copy-start.57 = (f32[512]{0:T(512)}, f32[512]{0:T(512)S(1)}, u32[]{:S(2)}) copy-start(f32[512]{0:T(512)S(1)} %add_rsqrt_fusion.1) | copy-start | bytes 6148
  15.4 129.2 %copy-start.59 = (f32[512]{0:T(512)}, f32[512]{0:T(512)S(1)}, u32[]{:S(2)}) copy-start(f32[512]{0:T(512)S(1)} %get-tuple-element.123) | copy-start | bytes 6148
  85.8 19.4 %all-to-all-start = ((f32[16,32,128]{2,1,0:T(8,128)}), f32[16,32,128]{2,1,0:T(8,128)}, u32[]{:S(2)}, u32[]{:S(2)}) async-start(f32[16,32,128]{2,1,0:T(8,128)} %bitcast.176), calls=%async_computation | async-start | bytes 524288 | tf_op jit(solution)/shard_map/all_to_all | solution.py:59
  91.7 13.5 %copy-start.71 = (s32[16]{0:T(128)S(1)}, s32[16]{0:T(128)}, u32[]{:S(2)}) copy-start(s32[16]{0:T(128)} %get-tuple-element.100) | copy-start | bytes 196
  91.7 13.5 %copy-start.73 = (s32[16]{0:T(128)S(1)}, s32[16]{0:T(128)}, u32[]{:S(2)}) copy-start(s32[16]{0:T(128)} %get-tuple-element.101) | copy-start | bytes 196
  107.4 22.2 %all-to-all-start.1 = ((f32[16,32,128]{2,1,0:T(8,128)}), f32[16,32,128]{2,1,0:T(8,128)}, u32[]{:S(2)}, u32[]{:S(2)}) async-start(f32[16,32,128]{2,1,0:T(8,128)} %copy.106), calls=%async_computation.1 | async-start | bytes 524288 | tf_op jit(solution)/shard_map/all_to_all | solution.py:63
  129.6 59.0 %all-to-all-start.3 = ((f32[8,64,768]{2,1,0:T(8,128)}), f32[8,64,768]{2,1,0:T(8,128)}, u32[]{:S(2)}, u32[]{:S(2)}) async-start(f32[8,64,768]{2,1,0:T(8,128)} %bitcast.172), calls=%async_computation.3 | async-start | bytes 3145728 | tf_op jit(solution)/shard_map/all_to_all | solution.py:154
  144.6 127.0 %copy-start.47 = (f32[6,512]{1,0:T(8,128)}, f32[6,512]{1,0:T(8,128)S(1)}, u32[]{:S(2)}) copy-start(f32[6,512]{1,0:T(8,128)S(1)} %add.269) | copy-start | bytes 36868
  147.4 4.9 copy-start.35
  147.4 6.4 %copy-start.82 = (s32[4,1]{0,1:T(1,128)S(1)}, s32[4,1]{0,1:T(1,128)}, u32[]{:S(2)}) copy-start(s32[4,1]{0,1:T(1,128)} %copy-done.81) | copy-start | bytes 52
  147.4 6.9 %copy-start.87 = (s32[8]{0:T(128)S(1)}, s32[8]{0:T(128)}, u32[]{:S(2)}) copy-start(s32[8]{0:T(128)} %param.34) | copy-start | bytes 100
  152.3 42.3 %collective-permute-start = (f32[512,768]{1,0:T(8,128)}, f32[512,768]{1,0:T(8,128)}, u32[]{:S(2)}, u32[]{:S(2)}) collective-permute-start(f32[512,768]{1,0:T(8,128)} %fusion.69), channel_id=1, source_target_pairs={{0,1},{1,0},{2,3},{3,2},{4,5},{5,4},{6,7},{7,6},{8,9},{9,8},{10,11... | collective-permute-start | bytes 4718600 | tf_op jit(solution)/shard_map/ppermute | solution.py:29
  154.3 37.5 %copy-start.88 = (s32[8]{0:T(128)}, s32[8]{0:T(128)S(1)}, u32[]{:S(2)}) copy-start(s32[8]{0:T(128)S(1)} %get-tuple-element.108) | copy-start | bytes 100
  199.4 57.4 %copy-start.55 = (f32[512]{0:T(512)}, f32[512]{0:T(512)S(1)}, u32[]{:S(2)}) copy-start(f32[512]{0:T(512)S(1)} %add_rsqrt_fusion) | copy-start | bytes 6148
  199.4 7.3 %copy-start.39 = (f32[768,3072]{1,0:T(8,128)S(1)}, f32[768,3072]{1,0:T(8,128)}, u32[]{:S(2)}) copy-start(f32[768,3072]{1,0:T(8,128)} %all-gather.5.cloned.1.call-done) | copy-start | bytes 28311556
  206.8 8.4 %copy-start.90 = (f32[512,1536]{1,0:T(8,128)}, f32[512,1536]{1,0:T(8,128)S(1)}, u32[]{:S(2)}) copy-start(f32[512,1536]{1,0:T(8,128)S(1)} %fusion.24) | copy-start | bytes 9437188
  215.2 40.1 %copy-start.4 = (f32[512,768]{1,0:T(8,128)S(1)}, f32[512,768]{1,0:T(8,128)}, u32[]{:S(2)}) copy-start(f32[512,768]{1,0:T(8,128)} %copy-done.3) | copy-start | bytes 4718596
  219.2 37.5 %copy-start.16 = (f32[8,64,768]{2,1,0:T(8,128)S(1)}, f32[8,64,768]{2,1,0:T(8,128)}, u32[]{:S(2)}) copy-start(f32[8,64,768]{2,1,0:T(8,128)} %gather_fusion.1) | copy-start | bytes 4718596
  219.2 36.1 %collective-permute-start.2 = (f32[512,768]{1,0:T(8,128)S(1)}, f32[512,768]{1,0:T(8,128)S(1)}, u32[]{:S(2)}, u32[]{:S(2)}) collective-permute-start(f32[512,768]{1,0:T(8,128)S(1)} %fusion.14), channel_id=1, source_target_pairs={{0,1},{1,0},{2,3},{3,2},{4,5},{5,4},{6,7},{7,6},{8,9},{9,8},{10,11... | collective-permute-start | bytes 4718600 | tf_op jit(solution)/shard_map/ppermute | solution.py:29
  264.6 6.8 %copy-start.19 = (f32[512,384]{0,1:T(8,128)}, f32[512,384]{0,1:T(8,128)S(1)}, u32[]{:S(2)}) copy-start(f32[512,384]{0,1:T(8,128)S(1)} %fusion.67) | copy-start | bytes 2359300
  265.6 5.9 %copy-start.46 = (f32[6,512,64]{1,2,0:T(8,128)S(1)}, f32[6,512,64]{1,2,0:T(8,128)}, u32[]{:S(2)}) copy-start(f32[6,512,64]{1,2,0:T(8,128)} %get-tuple-element.137) | copy-start | bytes 2359300
  274.6 18.4 %all-to-all-start.4 = ((f32[16,32,128]{2,1,0:T(8,128)}), f32[16,32,128]{2,1,0:T(8,128)}, u32[]{:S(2)}, u32[]{:S(2)}) async-start(f32[16,32,128]{2,1,0:T(8,128)} %bitcast.175), calls=%async_computation.4 | async-start | bytes 524288 | tf_op jit(solution)/shard_map/all_to_all | solution.py:59
  279.1 5.5 copy-start.20
  279.1 5.5 copy-start.48
  279.1 5.5 copy-start.50
  279.1 5.5 copy-start.51
  279.1 5.5 copy-start.61
  279.1 5.5 copy-start.63
  279.1 6.5 %copy-start.9 = (f32[6,512,64]{1,2,0:T(8,128)S(1)}, f32[6,512,64]{1,2,0:T(8,128)}, u32[]{:S(2)}) copy-start(f32[6,512,64]{1,2,0:T(8,128)} %copy-done.6) | copy-start | bytes 2359300
  279.1 6.5 %copy-start.13 = (f32[6,512,64]{1,2,0:T(8,128)S(1)}, f32[6,512,64]{1,2,0:T(8,128)}, u32[]{:S(2)}) copy-start(f32[6,512,64]{1,2,0:T(8,128)} %copy-done.10) | copy-start | bytes 2359300
  288.8 4.2 copy-start.72
  295.2 15.9 %all-to-all-start.5 = ((f32[16,32,128]{2,1,0:T(8,128)}), f32[16,32,128]{2,1,0:T(8,128)}, u32[]{:S(2)}, u32[]{:S(2)}) async-start(f32[16,32,128]{2,1,0:T(8,128)} %copy.113), calls=%async_computation.5 | async-start | bytes 524288 | tf_op jit(solution)/shard_map/all_to_all | solution.py:63
  301.3 211.0 %reduce-scatter.3.cloned.1.call-start = ((), (), s32[]{:S(2)}) async-start(), calls=%async_computation.10 | async-start | bytes 5013504 | tf_op jit(solution)/shard_map/reduce_scatter | solution.py:49
  322.9 6.9 %copy-start.33 = (f32[768,384]{1,0:T(8,128)S(1)}, f32[768,384]{1,0:T(8,128)}, u32[]{:S(2)}) copy-start(f32[768,384]{1,0:T(8,128)} %fusion.157) | copy-start | bytes 3538948
  332.7 210.4 %reduce-scatter.5.cloned.1.call-start = ((), (), s32[]{:S(2)}) async-start(), calls=%async_computation.11 | async-start | bytes 10027008 | tf_op jit(solution)/shard_map/reduce_scatter | solution.py:49
  334.1 6.4 %copy-start.41 = (f32[512,768]{1,0:T(8,128)S(1)}, f32[512,768]{1,0:T(8,128)}, u32[]{:S(2)}) copy-start(f32[512,768]{1,0:T(8,128)} %fusion.42) | copy-start | bytes 4718596
  334.1 6.4 %copy-start.91 = (f32[512,1536]{1,0:T(8,128)S(1)}, f32[512,1536]{1,0:T(8,128)}, u32[]{:S(2)}) copy-start(f32[512,1536]{1,0:T(8,128)} %copy-done.90) | copy-start | bytes 9437188
  362.7 4.4 copy-start.84
  363.9 20.7 %copy-start.80 = (f32[768]{0:T(1024)S(1)}, f32[768]{0:T(1024)}, u32[]{:S(2)}) copy-start(f32[768]{0:T(1024)} %param.32) | copy-start | bytes 9220
  364.8 19.7 %collective-permute-start.1 = (f32[8,32,768]{2,1,0:T(8,128)}, f32[8,32,768]{2,1,0:T(8,128)}, u32[]{:S(2)}, u32[]{:S(2)}) collective-permute-start(f32[8,32,768]{2,1,0:T(8,128)} %constant_dynamic-slice_fusion.1), channel_id=1, source_target_pairs={{0,1},{1,0},{2,3},{3,2},{4,5},{5,4},{6,7},{7,6},{8,9},{9,8},{10,11... | collective-permute-start | bytes 2359304 | tf_op jit(solution)/shard_map/ppermute | solution.py:210
  366.3 18.2 %copy-start.34 = (f32[512,768]{1,0:T(8,128)S(1)}, f32[512,768]{1,0:T(8,128)}, u32[]{:S(2)}) copy-start(f32[512,768]{1,0:T(8,128)} %get-tuple-element.111) | copy-start | bytes 4718596
  389.4 7.5 %copy-start.28 = (f32[6,512,64]{1,2,0:T(8,128)S(1)}, f32[6,512,64]{1,2,0:T(8,128)}, u32[]{:S(2)}) copy-start(f32[6,512,64]{1,2,0:T(8,128)} %copy-done.27) | copy-start | bytes 2359300
  390.4 65.9 %all-to-all-start.2 = ((f32[8,32,768]{2,1,0:T(8,128)}), f32[8,32,768]{2,1,0:T(8,128)}, u32[]{:S(2)}, u32[]{:S(2)}) async-start(f32[8,32,768]{2,1,0:T(8,128)} %broadcast_select_fusion), calls=%async_computation.2 | async-start | bytes 1572864 | tf_op jit(solution)/shard_map/all_to_all | solution.py:217
  398.6 11.8 %copy-start.31 = (f32[6,512,64]{1,2,0:T(8,128)S(1)}, f32[6,512,64]{1,2,0:T(8,128)}, u32[]{:S(2)}) copy-start(f32[6,512,64]{1,2,0:T(8,128)} %copy-done.30) | copy-start | bytes 2359300
  408.3 35.7 %collective-permute-start.8 = (f32[512,768]{1,0:T(8,128)}, f32[512,768]{1,0:T(8,128)}, u32[]{:S(2)}, u32[]{:S(2)}) collective-permute-start(f32[512,768]{1,0:T(8,128)} %fusion.21), channel_id=1, source_target_pairs={{0,1},{1,0},{2,3},{3,2},{4,5},{5,4},{6,7},{7,6},{8,9},{9,8},{10,11... | collective-permute-start | bytes 4718600 | tf_op jit(solution)/shard_map/ppermute | solution.py:29
  412.1 4.9 copy-start.68
  412.1 6.2 %copy-start.67 = (f32[768]{0:T(1024)S(1)}, f32[768]{0:T(1024)}, u32[]{:S(2)}) copy-start(f32[768]{0:T(1024)} %get-tuple-element.92) | copy-start | bytes 9220
  412.1 7.4 %copy-start.69 = (f32[1536]{0:T(1024)S(1)}, f32[1536]{0:T(1024)}, u32[]{:S(2)}) copy-start(f32[1536]{0:T(1024)} %get-tuple-element.138) | copy-start | bytes 18436
  420.8 28.6 %copy-start.37 = (f32[56576]{0:T(1024)S(1)}, f32[56576]{0:T(1024)}, u32[]{:S(2)}) copy-start(f32[56576]{0:T(1024)} %constant_dynamic-update-slice_fusion.1) | copy-start | bytes 678916
  447.7 44.8 %copy-start.15 = (f32[512,768]{1,0:T(8,128)S(1)}, f32[512,768]{1,0:T(8,128)}, u32[]{:S(2)}) copy-start(f32[512,768]{1,0:T(8,128)} %copy-done.14) | copy-start | bytes 4718596
  447.7 3.7 collective-permute-start.3
  451.5 1.6 collective-permute-start.4
  453.8 13.2 %collective-permute-start.5 = (f32[448,128]{1,0:T(8,128)}, f32[448,128]{1,0:T(8,128)}, u32[]{:S(2)}, u32[]{:S(2)}) collective-permute-start(f32[448,128]{1,0:T(8,128)} %fusion.146), channel_id=1, source_target_pairs={{0,16},{8,24},{16,0},{24,8},{1,17},{9,25},{17,1},{25,9},{2,18},{10... | collective-permute-start | bytes 688136 | tf_op jit(solution)/shard_map/ppermute | solution.py:39
  468.2 23.4 %collective-permute-start.6 = (f32[448,128]{1,0:T(8,128)S(1)}, f32[448,128]{1,0:T(8,128)S(1)}, u32[]{:S(2)}, u32[]{:S(2)}) collective-permute-start(f32[448,128]{1,0:T(8,128)S(1)} %fusion.178), channel_id=1, source_target_pairs={{0,2},{2,0},{4,6},{6,4},{1,3},{3,1},{5,7},{7,5},{8,10},{10,8},{12,... | collective-permute-start | bytes 688136 | tf_op jit(solution)/shard_map/ppermute | solution.py:39
  491.7 16.7 %collective-permute-start.7 = (f32[448,128]{1,0:T(8,128)S(1)}, f32[448,128]{1,0:T(8,128)S(1)}, u32[]{:S(2)}, u32[]{:S(2)}) collective-permute-start(f32[448,128]{1,0:T(8,128)S(1)} %add.308), channel_id=1, source_target_pairs={{0,4},{2,6},{4,0},{6,2},{1,5},{3,7},{5,1},{7,3},{8,12},{10,14},{12... | collective-permute-start | bytes 688136 | tf_op jit(solution)/shard_map/ppermute | solution.py:39
  513.3 33.8 %copy-start.1 = (f32[6,64,64]{2,1,0:T(8,128)S(1)}, f32[6,64,64]{2,1,0:T(8,128)}, u32[]{:S(2)}) copy-start(f32[6,64,64]{2,1,0:T(8,128)} %param.23) | copy-start | bytes 294916
  (49 other events, 102.5 us)
Sparse Core Ops, SparseCore 0:
  10.9 55.6 all-gather.2
  68.9 114.2 all-gather.4
  332.8 81.6 reduce-scatter.2
  418.5 124.6 reduce-scatter.4

commit v2 on v1

--- a/solution.py
+++ b/solution.py
@@ -1,6 +1,8 @@
 import jax
 import jax.numpy as jnp
 from jax import lax
+from jax.experimental import pallas as pl
+from jax.experimental.pallas import tpu as pltpu
 from jax.sharding import PartitionSpec as P
 
 HIGH = lax.Precision.HIGH
@@ -49,10 +51,130 @@
     return lax.psum_scatter(whole, DATA, scatter_dimension=0, tiled=True)
 
 
-def chain(state, normer, joins):
+def together(*values):
+    return lax.optimization_barrier(values)
+
+
+def small_grid():
+    return lax.axis_size("fsdp") == 4 and lax.axis_size("context") == 4
+
+
+def core_swap(part):
+    return lax.ppermute(part, "fsdp", [(i, i ^ 1) for i in range(4)])
+
+
+def side_swap(part):
+    return lax.ppermute(part, "fsdp", [(i, i ^ 2) for i in range(4)])
+
+
+def ring_next(part):
+    return lax.ppermute(part, "context", [(i, (i + 1) % 4) for i in range(4)])
+
+
+def put_in_order(parts, places):
+    number = len(parts)
+    rows, columns = parts[0].shape
+    inside = pl.BlockSpec(memory_space=pltpu.VMEM)
+
+    def kernel(at_ref, *refs):
+        out_ref = refs[number]
+        for i in range(number):
+            start = pl.multiple_of(at_ref[i] * rows, 8)
+            out_ref[pl.ds(start, rows), :] = refs[i][...]
+
+    return pl.pallas_call(
+        kernel,
+        out_shape=jax.ShapeDtypeStruct((number * rows, columns), jnp.float32),
+        in_specs=[pl.BlockSpec(memory_space=pltpu.SMEM)] + [inside] * number,
+        out_specs=inside,
+    )(places, *parts)
+
+
+def gather_ring(shard):
+    f, z = (lax.axis_index("fsdp"), lax.axis_index("context"))
+    owns, sides, parts = ([shard], [], [])
+    for k in range(4):
+        new = [side_swap(owns[k])]
+        if k < 3:
+            new.append(ring_next(owns[k]))
+        if k:
+            new += [core_swap(owns[k - 1]), core_swap(sides[k - 1])]
+        new = together(*new)
+        sides.append(new[0])
+        if k < 3:
+            owns.append(new[1])
+        parts += new[-2:] if k else []
+    parts += [core_swap(owns[3]), core_swap(sides[3])]
+    places = []
+    for who in (f, f ^ 2):
+        places += [who * 4 + (z - k) % 4 for k in range(4)]
+    for k in range(4):
+        places += [(who ^ 1) * 4 + (z - k) % 4 for who in (f, f ^ 2)]
+    return put_in_order(owns + sides + parts, jnp.stack(places).astype(jnp.int32))
+
+
+def take_at(array, index):
+    return lax.dynamic_index_in_dim(array, index, 0, False)
+
+
+def shift_down(array):
+    z = lax.axis_index("context")
+    total = take_at(array, z)
+    for k in (1, 2, 3):
+        pairs = [(i, (i + k) % 4) for i in range(4)]
+        total = total + lax.ppermute(take_at(array, (z + k) % 4), "context", pairs)
+    return total
+
+
+def side_down(array, axis):
+    x = lax.axis_index("fsdp") // 2
+    got = side_swap(lax.dynamic_index_in_dim(array, 1 - x, axis, False))
+    return lax.dynamic_index_in_dim(array, x, axis, False) + got
+
+
+def scatter_steps(whole, small, gated, early):
+    rows, columns = whole.shape
+    most = columns // 384 * 256
+    core = lax.axis_index("fsdp") % 2
+    cut = whole.reshape(2, 2, 4, rows // 16, columns)
+    got = core_swap(lax.dynamic_index_in_dim(cut, 1 - core, 1, False))
+    held = lax.dynamic_index_in_dim(cut, core, 1, False) + got
+    held, gated, early = together(held, gated, early)
+    other = lax.ppermute(gated, "tensor", [(0, 1), (1, 0)])
+    small = small + core_swap(small)
+    first = side_down(held[..., :most], 0)
+    second = shift_down(held[..., most:].transpose(1, 0, 2, 3))
+    small = small + side_swap(small)
+    first, second, small = together(first, second, small)
+    small = small + lax.ppermute(small, "context", [(i, i ^ 1) for i in range(4)])
+    own = [shift_down(first), side_down(second, 0)]
+    small = small + lax.ppermute(small, "context", [(i, i ^ 2) for i in range(4)])
+    own = jnp.concatenate(own, axis=-1)
+    own, small, other = together(own, small, other)
+    return own, small, gated + other, early
+
+
+def reach_of(rows):
+    longest = rows * lax.axis_size(DATA) // 4
+    return -(-(longest - 1) // rows)
+
+
+def chain(state, normer, joins, reach, reverse):
     heads, feats, head_dim = state.shape
     count = joins.shape[0]
     packed = jnp.concatenate([jnp.swapaxes(state, 1, 2), normer[:, None, :]], axis=1)
+    if reach <= 4:
+        me = lax.axis_index(DATA)
+        weights = lax.dynamic_index_in_dim(joins, me, 0, keepdims=False)
+        back = 0.0
+        for step in range(1, reach + 1):
+            pairs = [(i, i + step) for i in range(count - step)]
+            if reverse:
+                pairs = [(b, a) for a, b in pairs]
+            at = me + step if reverse else me - step
+            weight = lax.dynamic_index_in_dim(weights, jnp.clip(at, 0, count - 1), 0, False)
+            back = back + weight * lax.ppermute(packed, DATA, pairs)
+        return back[:, :head_dim], back[:, head_dim]
     lines = heads * (head_dim + 1)
     share = -(-lines // (8 * count)) * 8
     packed = jnp.pad(packed.reshape(lines, feats), ((0, share * count - lines), (0, 0)))
@@ -131,14 +253,13 @@
     lower = jnp.arange(rows)[:, None] >= jnp.arange(rows)[None, :]
     allowed = jnp.logical_and(lower, segment[:, None] == segment[None, :])
 
-    first_pack = jnp.concatenate([qkv_weight.reshape(-1, 3 * local), out_weight.T], axis=1)
-    second_pack = jnp.concatenate([up_weight, down_weight.T], axis=1)
-    first_full = gather_rows(first_pack)
-    second_full = gather_rows(second_pack)
-    qkv_full = first_full[:, : 3 * local]
-    out_full = first_full[:, 3 * local :]
-    up_full = second_full[:, :hidden_units]
-    down_full = second_full[:, hidden_units:]
+    first_shard = jnp.concatenate([qkv_weight.reshape(-1, 3 * local), out_weight.T], axis=1)
+    second_shard = jnp.concatenate([up_weight, down_weight.T], axis=1)
+    first_full = gather_ring(first_shard) if small_grid() else gather_rows(first_shard)
+    first_full, second_shard = together(first_full, second_shard)
+    second_full = gather_rows(second_shard)
+    qkv_full, out_full = (first_full[:, : 3 * local], first_full[:, 3 * local :])
+    up_full, down_full = (second_full[:, :hidden_units], second_full[:, hidden_units:])
 
     slots = deal.shape[0]
     group_rows = rows // slots
@@ -151,14 +272,6 @@
     source_of = jnp.sum(
         jnp.where(slot_of[None, :] == counting[:, None], counting[None, :], 0), axis=1
     )
-    inbound = lax.all_to_all(
-        cotangent.reshape(slots, group_rows, width),
-        "context",
-        split_axis=0,
-        concat_axis=0,
-        tiled=True,
-    )
-
     hat1, scale1 = row_stats(block_input)
     normed1 = hat1 * ln1_gain + ln1_shift
     qkv = dot(normed1, qkv_full, ((1,), (0,))) + qkv_bias.reshape(1, 3 * local)
@@ -176,16 +289,27 @@
     tail_k = phi_k * to_final[None, :, None]
     heads_b = ((0,), (0,))
     state_tail = dot(tail_k, values, ((1,), (1,)), heads_b)
-    state_in, norm_in = chain(state_tail, jnp.sum(tail_k, axis=1), joins)
+    state_in, norm_in = chain(
+        state_tail, jnp.sum(tail_k, axis=1), joins, reach_of(rows), False
+    )
     scores = jnp.where(allowed[None], dot(phi_q, phi_k, ((2,), (2,)), heads_b), 0.0)
     head_q = phi_q * from_first[None, :, None]
+    state_in, norm_in, cotangent = together(state_in, norm_in, cotangent)
+    inbound = lax.all_to_all(
+        cotangent.reshape(slots, group_rows, width),
+        "context",
+        split_axis=0,
+        concat_axis=0,
+        tiled=True,
+    )
     numer = dot(scores, values, ((2,), (1,)), heads_b) + dot(
         head_q, state_in, ((2,), (2,)), heads_b
     )
     denom = jnp.sum(scores, axis=2) + jnp.sum(head_q * norm_in[:, None, :], axis=2)
     attended = numer / denom[:, :, None]
     flat = attended.transpose(1, 0, 2).reshape(rows, local)
-    attn = tensor_sum(dot(flat, out_full, ((1,), (1,)))) + out_bias
+    attn_terms = dot(flat, out_full, ((1,), (1,)))
+    attn = tensor_sum(attn_terms) + out_bias
     hidden = block_input + attn
 
     hat2, scale2 = row_stats(hidden)
@@ -198,11 +322,21 @@
     )
     mlp_terms = dot(active, down_full, ((1,), (1,)))
 
+    grad_y = jnp.take(inbound, slot_of, axis=0).reshape(rows, width) * valid
+    down_grad = dot(grad_y, active, ((0,), (0,)))
+    grad_pre = dot(grad_y, down_full, ((1,), (0,))) * slope
+    grad_normed2 = tensor_sum(dot(grad_pre, up_full, ((1,), (1,))))
+    second_grad = jnp.concatenate([dot(normed2, grad_pre, ((0,), (0,))), down_grad], axis=1)
+    second_own = scatter_rows(second_grad)
+    grad_normed2 = grad_normed2 + 0.0 * second_grad[:1, :1]
+    grad_hidden = grad_y + norm_backward(grad_normed2, hat2, scale2, ln2_gain)
+
     def own_part(array):
         return lax.dynamic_slice_in_dim(
             array.reshape(slots, group_rows, width), part_start, part_rows, 1
         )
 
+    mlp_terms = mlp_terms + 0.0 * grad_normed2[:1, :1]
     if tensor == 2:
         other = lax.dynamic_slice_in_dim(
             mlp_terms.reshape(slots, group_rows, width), part_rows - part_start, part_rows, 1
@@ -214,7 +348,6 @@
     attn_own = own_part(attn)
     result = own_part(hidden) + mlp_own
     outbound = jnp.take(result, source_of, axis=0)
-    dealt_output = lax.all_to_all(outbound, "context", split_axis=0, concat_axis=0, tiled=True)
     weight_own = own_part(jnp.broadcast_to(valid, (rows, width)))[:, :, :1]
     squares = jnp.stack(
         [
@@ -224,15 +357,6 @@
         ]
     )
 
-    grad_y = jnp.take(inbound, slot_of, axis=0).reshape(rows, width) * valid
-    grad_pre = dot(grad_y, down_full, ((1,), (0,))) * slope
-    grad_normed2 = tensor_sum(dot(grad_pre, up_full, ((1,), (1,))))
-    second_grad = jnp.concatenate(
-        [dot(normed2, grad_pre, ((0,), (0,))), dot(grad_y, active, ((0,), (0,)))], axis=1
-    )
-    second_own = scatter_rows(second_grad)
-    grad_hidden = grad_y + norm_backward(grad_normed2, hat2, scale2, ln2_gain)
-
     out_grad = dot(grad_hidden, flat, ((0,), (0,)))
     grad_flat = dot(grad_hidden, out_full, ((1,), (0,)))
     grad_attended = grad_flat.reshape(rows, heads, head_dim).transpose(1, 0, 2)
@@ -240,7 +364,11 @@
     grad_denom = -jnp.sum(grad_attended * attended, axis=2) / denom
     state_grad_in = dot(head_q, grad_numer, ((1,), (1,)), heads_b)
     norm_grad_in = jnp.sum(head_q * grad_denom[:, :, None], axis=1)
-    state_grad, norm_grad = chain(state_grad_in, norm_grad_in, joins.T)
+    state_grad, norm_grad = chain(
+        state_grad_in, norm_grad_in, joins.T, reach_of(rows), True
+    )
+    state_grad, norm_grad, outbound = together(state_grad, norm_grad, outbound)
+    dealt_output = lax.all_to_all(outbound, "context", split_axis=0, concat_axis=0, tiled=True)
     pulls = jnp.where(
         allowed[None],
         dot(grad_numer, values, ((2,), (2,)), heads_b) + grad_denom[:, :, None],
@@ -274,12 +402,10 @@
         .transpose(2, 0, 1, 3)
         .reshape(rows, 3 * local)
     )
-    grad_normed1_part = dot(grad_qkv, qkv_full, ((1,), (1,)))
     first_grad = jnp.concatenate([dot(normed1, grad_qkv, ((0,), (0,))), out_grad], axis=1)
-    first_own = scatter_rows(first_grad)
-    grad_normed1 = tensor_sum(grad_normed1_part)
-    grad_input = grad_hidden + norm_backward(grad_normed1, hat1, scale1, ln1_gain)
-
+    grad_normed1_part = dot(
+        grad_qkv + 0.0 * first_grad[:1, :1], qkv_full, ((1,), (1,))
+    )
     crossing = tensor_sum(
         jnp.concatenate(
             [
@@ -301,8 +427,17 @@
         crossing,
     ]
     joined = jnp.concatenate(small)
-    joined = jnp.pad(joined, (0, -joined.shape[0] % 1024))
-    total = data_sum(joined.reshape(-1, 128)).reshape(-1)
+    joined = jnp.pad(joined, (0, -joined.shape[0] % 1024)).reshape(-1, 128)
+    if small_grid() and tensor == 2:
+        first_own, total, grad_normed1, dealt_output = scatter_steps(
+            first_grad, joined, grad_normed1_part, dealt_output
+        )
+    else:
+        first_own = scatter_rows(first_grad)
+        total = data_sum(joined)
+        grad_normed1 = tensor_sum(grad_normed1_part)
+    total = total.reshape(-1)
+    grad_input = grad_hidden + norm_backward(grad_normed1, hat1, scale1, ln1_gain)
     pieces = []
     at = 0
     for part in small:

time: 564 us -> 469 us (0.83)
  waiting for transfers between devices: 256 us -> 129 us
  starting transfers between devices: 40.7 us -> 79.8 us
  matrix products: 132 us -> 111 us
  other arithmetic: 58.6 us -> 65.7 us
    all_gather x2 -> x1, waiting for transfers between devices: 50.3 us -> 0.01 us  [gather_rows(): return lax.all_gather(shard, DATA, axis=0, tiled=True)]
    ppermute x4 -> x3, waiting for transfers between devices: 59.8 us -> 19.1 us  [tensor_sum(): part = part + lax.ppermute(part, 'tensor', swap_with('tensor', bit))]
    ppermute x4 -> x37, starting transfers between devices: 4.62 us -> 45.1 us  [the longest x8 17.5 us: chain(): back = back + weight * lax.ppermute(packed, DATA, pairs)]
    reduce_scatter x2 -> x1, waiting for transfers between devices: 27.6 us -> 0.01 us  [scatter_rows(): return lax.psum_scatter(whole, DATA, scatter_dimension=0, tiled=True)]
    ppermute x4 -> x37, waiting for transfers between devices: 46.5 us -> 71.2 us  [the longest x3 25.6 us: ring_next(): return lax.ppermute(part, 'context', [(i, (i + 1) % 4) for i in range(4)])]
    all_to_all x4 -> x0, waiting for transfers between devices: 22.4 us -> none  [the longest x2 11.4 us: chain(): lax.all_to_all(packed.reshape(count, share, feats), DATA, split_axis=0, c...]
    dot_general x32 -> x30, matrix products: 132 us -> 111 us  [dot(): lax.dot_general(a, b, (over, batch), precision=precision, preferred_eleme...]
    all_to_all x4 -> x0, starting transfers between devices: 18.9 us -> none  [the longest x2 10.3 us: chain(): lax.all_to_all(joined.reshape(count, share, feats), DATA, split_axis=0, c...]
  transfers between devices with their start and end apart: 19 -> 45, of which waited for: 14 -> 13; matrix products, arithmetic and copies ran while one was open for 30% -> 41% of each run, Pallas kernels for 0% -> 0%
where the time goes in v2:
time: 469 us; the launch traced here: 460 us
  waiting for transfers between devices  129 us (28%)
  matrix products  111 us (24%)
  starting transfers between devices  79.8 us (17%)
  other arithmetic  65.7 us (14%)
  local copies, waits for them, and re-layouts  51 us (11%)
  between operations  18.8 us (4%)
  Pallas kernels  4.89 us (1%)
    dot_general x30, matrix products, dot(): lax.dot_general(a, b, (over, batch), precision=precision, preferred_eleme...  111 us
    all_to_all x1, waiting for transfers between devices, body(): lax.all_to_all(cotangent.reshape(slots, group_rows, width), 'context', sp...  38.7 us
    ppermute x3, waiting for transfers between devices, ring_next(): return lax.ppermute(part, 'context', [(i, (i + 1) % 4) for i in range(4)])  25.6 us
    ppermute x7, waiting for transfers between devices, side_swap(): return lax.ppermute(part, 'fsdp', [(i, i ^ 2) for i in range(4)])  21.6 us
    ppermute x3, waiting for transfers between devices, tensor_sum(): part = part + lax.ppermute(part, 'tensor', swap_with('tensor', bit))  19.1 us
    all_to_all x1, starting transfers between devices, body(): lax.all_to_all(cotangent.reshape(slots, group_rows, width), 'context', sp...  18.3 us
    ppermute x8, starting transfers between devices, chain(): back = back + weight * lax.ppermute(packed, DATA, pairs)  17.5 us
    unnamed x225, local copies, waits for them, and re-layouts  15.7 us
  transfers between devices with their start and end apart: 45, of which 13 were waited for; matrix products, arithmetic and copies ran while one was open for 41% of the time, Pallas kernels for 0%

profile of v2, /device:TPU:0, one launch (start us, length us, event | category | flops | bytes accessed | tf_op | source)
XLA Modules:
  0.0 460.5 jit_solution(14824436657627866837)
XLA Ops:
  9.2 3.1 collective-permute-start.1
  13.8 7.5 %collective-permute-done.1.refs_1_ = f32[48,1536]{1,0:T(8,128)S(1)} collective-permute-done((f32[48,1536]{1,0:T(8,128)S(1)}, f32[48,1536]{1,0:T(8,128)S(1)}, u32[]{:S(2)}, u32[]{:S(2)}) %collective-permute-start.1) | collective-permute-done | bytes 294944 | tf_op jit(solution)/shard_map/ppermute | solution.py:71
  23.8 8.7 %collective-permute-done.3.refs_2_ = f32[48,1536]{1,0:T(8,128)S(1)} collective-permute-done((f32[48,1536]{1,0:T(8,128)S(1)}, f32[48,1536]{1,0:T(8,128)S(1)}, u32[]{:S(2)}, u32[]{:S(2)}) %collective-permute-start.3) | collective-permute-done | bytes 294944 | tf_op jit(solution)/shard_map/ppermute | solution.py:71
  34.6 9.3 %collective-permute-done.7.refs_3_ = f32[48,1536]{1,0:T(8,128)S(1)} collective-permute-done((f32[48,1536]{1,0:T(8,128)S(1)}, f32[48,1536]{1,0:T(8,128)S(1)}, u32[]{:S(2)}, u32[]{:S(2)}) %collective-permute-start.7) | collective-permute-done | bytes 294944 | tf_op jit(solution)/shard_map/ppermute | solution.py:71
  46.3 7.1 %collective-permute-done.10.refs_7_ = f32[48,1536]{1,0:T(8,128)} collective-permute-done((f32[48,1536]{1,0:T(8,128)S(1)}, f32[48,1536]{1,0:T(8,128)}, u32[]{:S(2)}, u32[]{:S(2)}) %collective-permute-start.10) | collective-permute-done | bytes 294944 | tf_op jit(solution)/shard_map/ppermute | solution.py:67
  53.5 1.9 pad_maximum_fusion.5
  55.5 4.9 %shard_map.305 = f32[768,1536]{1,0:T(8,128)} custom-call(s32[16]{0:T(128)} %stack.91.at_ref, f32[48,1536]{1,0:T(8,128)} %copy-done.49, f32[48,1536]{1,0:T(8,128)} %copy-done.56, f32[48,1536]{1,0:T(8,128)} %copy-done.60, f32[48,1536]{1,0:T(8,128)} %copy-done.64, f32[48,1536]{1,0:T(8,128)} %copy-done.57, f32[48,1536]{1,0:T(8,128)} %copy-done.61, ...), custom_call_target="tpu_custom_call" | custom-call | tf_op jit(solution)/shard_map/pallas_call | solution.py:85
  64.9 6.8 %convolution_add_fusion = f32[512,1152]{1,0:T(8,128)} fusion(f32[768,1536]{1,0:T(8,128)} %shard_map.305, f32[1152]{0:T(1024)S(1)} %add.532, f32[512,768]{1,0:T(8,128)S(1)} %copy-done.1, f32[768]{0:T(1024)S(1)} %copy-done.92, f32[768]{0:T(1024)S(1)} %copy-done.83, f32[512]{0:T(512)S(1)} %add_rsqrt_fusion.1, f32[512]{0:T(512)S(1)} %broadcast_multiply_fusion.5), kind=kOutput, calls=%fused_computation.26 | convolution fusion | flops 2720071680 | bytes 7485952 | tf_op jit(solution)/shard_map/dot_general | solution.py:17
  71.8 3.1 copy.69
  74.9 1.7 fusion.100
  81.8 2.5 collective-permute-start.18
  84.2 3.5 collective-permute-start.17
  89.1 4.1 collective-permute-start.15
  97.2 3.2 select_reduce_fusion
  100.5 2.5 fusion.8
  103.1 2.7 multiply_add_fusion.12
  106.2 2.2 bitcast_divide_fusion
  108.4 4.9 %fusion.71 = f32[512,768]{1,0:T(8,128)} fusion(f32[512,384]{0,1:T(8,128)S(1)} %bitcast.204, f32[768,1536]{1,0:T(8,128)} %shard_map.305), kind=kOutput, calls=%fused_computation.108 | convolution fusion | flops 905969664 | bytes 3538944 | tf_op jit(solution)/shard_map/dot_general | solution.py:17
  115.5 18.3 %all-to-all-start = ((f32[8,64,768]{2,1,0:T(8,128)}), f32[8,64,768]{2,1,0:T(8,128)}, u32[]{:S(2)}, u32[]{:S(2)}) async-start(f32[8,64,768]{2,1,0:T(8,128)} %bitcast.208), calls=%async_computation | async-start | bytes 3145728 | tf_op jit(solution)/shard_map/all_to_all | solution.py:298
  137.1 1.9 collective-permute-done.19
  138.9 3.3 fusion.141
  143.7 38.7 %all-to-all-done = f32[8,64,768]{2,1,0:T(8,128)} async-done(((f32[8,64,768]{2,1,0:T(8,128)}), f32[8,64,768]{2,1,0:T(8,128)}, u32[]{:S(2)}, u32[]{:S(2)}) %all-to-all-start) | async-done | bytes 1572896 | tf_op jit(solution)/shard_map/all_to_all | solution.py:298
  182.3 3.2 gather_fusion
  185.5 2.8 fusion.43
  188.4 7.1 %fusion.24 = f32[512,1536]{1,0:T(8,128)S(1)} fusion(f32[768,3072]{1,0:T(8,128)} %all-gather.2.cloned.1.call-done, f32[1536]{0:T(1024)S(1)} %copy-done.97, f32[512,768]{1,0:T(8,128)} %copy-done.4, f32[768]{0:T(1024)S(1)} %copy-done.89, f32[768]{0:T(1024)S(1)} %copy-done.75, f32[512]{0:T(512)S(1)} %add_rsqrt_fusion, f32[512]{0:T(512)S(1)} %broadcast_multiply_fusion.4), kind=kOutput, calls=%fused_computation.31 | convolution fusion | flops 3626237952 | bytes 9453568 | tf_op jit(solution)/shard_map/dot_general | solution.py:17
  195.5 8.4 %fusion.150 = (f32[1536]{0:T(1024)}, f32[512,1536]{1,0:T(8,128)S(1)}) fusion(f32[512,1536]{1,0:T(8,128)S(1)} %fusion.24, f32[512,768]{1,0:T(8,128)} %fusion.43, f32[768,3072]{1,0:T(8,128)S(1)} %copy-done.44), kind=kOutput, calls=%fused_computation.294 | convolution fusion | flops 3638819328 | bytes 12589056 | tf_op jit(solution)/shard_map/dot_general | solution.py:17
  203.9 5.2 %fusion.10 = f32[512,768]{1,0:T(8,128)} fusion(f32[512,1536]{1,0:T(8,128)S(1)} %get-tuple-element.179, f32[768,3072]{1,0:T(8,128)S(1)} %copy-done.44), kind=kOutput, calls=%fused_computation.18 | convolution fusion | flops 3623878656 | bytes 9437184 | tf_op jit(solution)/shard_map/dot_general | solution.py:17
  211.4 4.6 %fusion.50 = f32[768,1536]{1,0:T(8,128)S(1)} fusion(f32[512,1536]{1,0:T(8,128)S(1)} %get-tuple-element.179, f32[512,768]{1,0:T(8,128)S(1)} %copy-done.5, f32[768]{0:T(1024)S(1)} %copy-done.89, f32[768]{0:T(1024)S(1)} %copy-done.75, f32[512]{0:T(512)S(1)} %add_rsqrt_fusion, f32[512]{0:T(512)S(1)} %broadcast_multiply_fusion.4), kind=kOutput, calls=%fused_computation.83 | convolution fusion | flops 3625451520 | bytes 9447424 | tf_op jit(solution)/shard_map/dot_general | solution.py:17
  216.6 6.2 %fusion.44 = f32[768,1536]{1,0:T(8,128)} fusion(f32[512,768]{1,0:T(8,128)S(1)} %copy-done.47, f32[512,1536]{1,0:T(8,128)S(1)} %fusion.24), kind=kOutput, calls=%fused_computation.77 | convolution fusion | flops 3630170112 | bytes 9437184 | tf_op jit(solution)/shard_map/dot_general | solution.py:17
  222.8 7.0 %pad_maximum_fusion = f32[768,3072]{1,0:T(8,128)} fusion(f32[768,1536]{1,0:T(8,128)} %fusion.44, f32[768,1536]{1,0:T(8,128)S(1)} %fusion.50), kind=kLoop, calls=%fused_computation.6 | loop fusion | flops 2359296 | bytes 18874368 | tf_op jit(solution)/shard_map/concatenate | solution.py:329
  230.5 15.2 %collective-permute-done.20 = f32[512,768]{1,0:T(8,128)} collective-permute-done((f32[512,768]{1,0:T(8,128)}, f32[512,768]{1,0:T(8,128)}, u32[]{:S(2)}, u32[]{:S(2)}) %collective-permute-start.20) | collective-permute-done | bytes 1572896 | tf_op jit(solution)/shard_map/ppermute | solution.py:31
  245.7 4.5 multiply_reduce_fusion.3
  252.4 3.0 fusion.69
  262.5 1.7 collective-permute-start.21
  264.3 2.7 fusion.103
  267.6 4.7 %broadcast_add_fusion = f32[512,768]{1,0:T(8,128)S(1)} fusion(f32[]{:T(128)} %bitcast.48, f32[768,3072]{1,0:T(8,128)S(1)} %bitcast.207, f32[512,1536]{1,0:T(8,128)S(1)} %copy-done.101), kind=kOutput, calls=%fused_computation.125 | convolution fusion | flops 3630563328 | bytes 9437188 | tf_op jit(solution)/shard_map/dot_general | solution.py:17
  275.2 2.6 fusion.5
  282.1 8.1 %fusion.4 = f32[6,512,128]{1,2,0:T(8,128)} fusion(f32[6,512,512]{1,2,0:T(8,128)} %copy-done.2, f32[6,512]{1,0:T(8,128)} %copy-done.66, pred[512,512]{0,1:T(8,128)(4,1)} %fusion.73, f32[6,512,64]{1,2,0:T(8,128)} %copy-done.8, f32[6,512,64]{1,2,0:T(8,128)} %copy-done.10), kind=kOutput, calls=%fused_computation.8 | convolution fusion | flops 1211498496 | bytes 9711616 | tf_op jit(solution)/shard_map/dot_general | solution.py:17
  290.2 7.1 %fusion.6 = f32[6,512,64]{1,2,0:T(8,128)} fusion(f32[6,512,512]{1,2,0:T(8,128)} %copy-done.3, pred[512,512]{0,1:T(8,128)(4,1)S(1)} %copy-done.25, f32[6,512,64]{1,2,0:T(8,128)S(1)} %bitcast.202, f32[6,512]{1,0:T(8,128)S(1)} %add.549), kind=kOutput, calls=%fused_computation.10 | convolution fusion | flops 605749248 | bytes 8138752 | tf_op jit(solution)/shard_map/dot_general | solution.py:17
  297.9 3.7 fusion.151
  303.0 3.6 multiply_add_fusion.11
  306.7 2.9 fusion.74
  309.6 2.7 gather_fusion.1
  312.3 2.2 broadcast_select_fusion
  314.5 10.3 %all-to-all-start.1 = ((f32[8,32,768]{2,1,0:T(8,128)}), f32[8,32,768]{2,1,0:T(8,128)}, u32[]{:S(2)}, u32[]{:S(2)}) async-start(f32[8,32,768]{2,1,0:T(8,128)} %broadcast_select_fusion), calls=%async_computation.1 | async-start | bytes 1572864 | tf_op jit(solution)/shard_map/all_to_all | solution.py:371
  324.8 2.6 multiply_add_fusion.2
  332.2 6.7 %fusion.49 = f32[768,1152]{1,0:T(8,128)S(1)} fusion(f32[512,1152]{0,1:T(8,128)S(1)} %bitcast.192, f32[512,768]{1,0:T(8,128)S(1)} %copy-done.1, f32[768]{0:T(1024)S(1)} %copy-done.93, f32[768]{0:T(1024)S(1)} %copy-done.84, f32[512]{0:T(512)S(1)} %copy-done.74, f32[512]{0:T(512)S(1)} %copy-done.70), kind=kOutput, calls=%fused_computation.82 | convolution fusion | flops 2719481856 | bytes 7481344 | tf_op jit(solution)/shard_map/dot_general | solution.py:17
  340.1 1.7 dynamic-slice_bitcast_fusion
  343.0 1.8 fusion.99
  347.6 2.0 select_maximum_fusion
  349.7 9.1 %multiply_reduce_fusion.1 = (f32[768]{0:T(1024)S(1)}, f32[768]{0:T(1024)S(1)}, f32[512,768]{1,0:T(8,128)S(1)}) fusion(f32[512,768]{1,0:T(8,128)S(1)} %copy-done.1, f32[512]{0:T(512)S(1)} %copy-done.74, f32[512]{0:T(512)S(1)} %copy-done.70, f32[768,1536]{1,0:T(8,128)} %shard_map.305, f32[512,1152]{0,1:T(8,128)} %bitcast.193, f32[]{:T(128)} %bitcast.60), kind=kOutput, calls=%fused_computation.60 | convolution fusion | flops 2720463360 | bytes 9054720 | tf_op jit(solution)/shard_map/dot_general | solution.py:17
  360.5 2.0 collective-permute-done.31
  364.0 3.5 bitcast_add_fusion
  376.8 3.0 collective-permute-start.28
  381.7 14.5 %collective-permute-done.33 = f32[448,128]{1,0:T(8,128)} collective-permute-done((f32[448,128]{1,0:T(8,128)}, f32[448,128]{1,0:T(8,128)}, u32[]{:S(2)}, u32[]{:S(2)}) %collective-permute-start.33) | collective-permute-done | bytes 229408 | tf_op jit(solution)/shard_map/ppermute | solution.py:67
  401.2 2.4 collective-permute-start.38
  403.7 3.8 collective-permute-start.36
  407.9 8.1 %collective-permute-done.34 = f32[48,1024]{1,0:T(8,128)S(1)} collective-permute-done((f32[48,1024]{1,0:T(8,128)S(1)}, f32[48,1024]{1,0:T(8,128)S(1)}, u32[]{:S(2)}, u32[]{:S(2)}) %collective-permute-start.34) | collective-permute-done | bytes 196640 | tf_op jit(solution)/shard_map/ppermute | solution.py:125
  415.9 4.7 %collective-permute-done.36 = f32[48,1024]{1,0:T(8,128)S(1)} collective-permute-done((f32[48,1024]{1,0:T(8,128)S(1)}, f32[48,1024]{1,0:T(8,128)S(1)}, u32[]{:S(2)}, u32[]{:S(2)}) %collective-permute-start.36) | collective-permute-done | bytes 196640 | tf_op jit(solution)/shard_map/ppermute | solution.py:125
  420.6 2.7 collective-permute-done.35
  424.9 8.5 %collective-permute-done.39 = f32[448,128]{1,0:T(8,128)S(1)} collective-permute-done((f32[448,128]{1,0:T(8,128)S(1)}, f32[448,128]{1,0:T(8,128)S(1)}, u32[]{:S(2)}, u32[]{:S(2)}) %collective-permute-start.39) | collective-permute-done | bytes 229408 | tf_op jit(solution)/shard_map/ppermute | solution.py:151
  440.0 2.1 fusion.139
  449.2 1.9 slice_bitcast_fusion.11
  451.1 2.1 copy.118
  (408 shorter events, 97.1 us)
Async XLA Ops:
  7.2 86.0 %copy-start = (f32[6,64,64]{2,1,0:T(8,128)S(1)}, f32[6,64,64]{2,1,0:T(8,128)}, u32[]{:S(2)}) copy-start(f32[6,64,64]{2,1,0:T(8,128)} %param.23) | copy-start | bytes 294916
  7.2 181.2 %all-gather.2.cloned.1.call-start = ((), (), s32[]{:S(2)}) async-start(), calls=%async_computation.3 | async-start | bytes 10027008 | tf_op jit(solution)/shard_map/all_gather | solution.py:47
  9.2 46.3 %copy-start.49 = (f32[48,1536]{1,0:T(8,128)}, f32[48,1536]{1,0:T(8,128)S(1)}, u32[]{:S(2)}) copy-start(f32[48,1536]{1,0:T(8,128)S(1)} %pad_maximum_fusion.10.refs_0_) | copy-start | bytes 884740
  9.2 12.1 %collective-permute-start.1 = (f32[48,1536]{1,0:T(8,128)S(1)}, f32[48,1536]{1,0:T(8,128)S(1)}, u32[]{:S(2)}, u32[]{:S(2)}) collective-permute-start(f32[48,1536]{1,0:T(8,128)S(1)} %pad_maximum_fusion.10.refs_0_), channel_id=1, source_target_pairs={{0,2},{2,4},{4,6},{6,0},{1,3},{3,5},{5,7},{7,1},{8,10},{10,12},{12... | collective-permute-start | bytes 884744 | tf_op jit(solution)/shard_map/ppermute | solution.py:71
  12.3 9.0 %collective-permute-start = (f32[48,1536]{1,0:T(8,128)S(1)}, f32[48,1536]{1,0:T(8,128)S(1)}, u32[]{:S(2)}, u32[]{:S(2)}) collective-permute-start(f32[48,1536]{1,0:T(8,128)S(1)} %pad_maximum_fusion.10.refs_0_), channel_id=1, source_target_pairs={{0,16},{8,24},{16,0},{24,8},{1,17},{9,25},{17,1},{25,9},{2,18},{10... | collective-permute-start | bytes 884744 | tf_op jit(solution)/shard_map/ppermute | solution.py:67
  13.8 10.1 %collective-permute-start.4 = (f32[48,1536]{1,0:T(8,128)S(1)}, f32[48,1536]{1,0:T(8,128)S(1)}, u32[]{:S(2)}, u32[]{:S(2)}) collective-permute-start(f32[48,1536]{1,0:T(8,128)S(1)} %pad_maximum_fusion.10.refs_0_), channel_id=1, source_target_pairs={{0,8},{8,0},{16,24},{24,16},{1,9},{9,1},{17,25},{25,17},{2,10},{10... | collective-permute-start | bytes 884744 | tf_op jit(solution)/shard_map/ppermute | solution.py:63
  21.3 34.2 %copy-start.56 = (f32[48,1536]{1,0:T(8,128)}, f32[48,1536]{1,0:T(8,128)S(1)}, u32[]{:S(2)}) copy-start(f32[48,1536]{1,0:T(8,128)S(1)} %collective-permute-done.1.refs_1_) | copy-start | bytes 884740
  21.3 34.2 %copy-start.57 = (f32[48,1536]{1,0:T(8,128)}, f32[48,1536]{1,0:T(8,128)S(1)}, u32[]{:S(2)}) copy-start(f32[48,1536]{1,0:T(8,128)S(1)} %collective-permute-done.refs_4_) | copy-start | bytes 884740
  21.3 2.5 collective-permute-start.5
  21.4 11.2 %collective-permute-start.3 = (f32[48,1536]{1,0:T(8,128)S(1)}, f32[48,1536]{1,0:T(8,128)S(1)}, u32[]{:S(2)}, u32[]{:S(2)}) collective-permute-start(f32[48,1536]{1,0:T(8,128)S(1)} %collective-permute-done.1.refs_1_), channel_id=1, source_target_pairs={{0,2},{2,4},{4,6},{6,0},{1,3},{3,5},{5,7},{7,1},{8,10},{10,12},{12... | collective-permute-start | bytes 884744 | tf_op jit(solution)/shard_map/ppermute | solution.py:71
  22.3 10.3 %collective-permute-start.2 = (f32[48,1536]{1,0:T(8,128)S(1)}, f32[48,1536]{1,0:T(8,128)S(1)}, u32[]{:S(2)}, u32[]{:S(2)}) collective-permute-start(f32[48,1536]{1,0:T(8,128)S(1)} %collective-permute-done.1.refs_1_), channel_id=1, source_target_pairs={{0,16},{8,24},{16,0},{24,8},{1,17},{9,25},{17,1},{25,9},{2,18},{10... | collective-permute-start | bytes 884744 | tf_op jit(solution)/shard_map/ppermute | solution.py:67
  23.8 10.7 %collective-permute-start.8 = (f32[48,1536]{1,0:T(8,128)S(1)}, f32[48,1536]{1,0:T(8,128)S(1)}, u32[]{:S(2)}, u32[]{:S(2)}) collective-permute-start(f32[48,1536]{1,0:T(8,128)S(1)} %collective-permute-done.1.refs_1_), channel_id=1, source_target_pairs={{0,8},{8,0},{16,24},{24,16},{1,9},{9,1},{17,25},{25,17},{2,10},{10... | collective-permute-start | bytes 884744 | tf_op jit(solution)/shard_map/ppermute | solution.py:63
  23.8 31.7 %copy-start.58 = (f32[48,1536]{1,0:T(8,128)}, f32[48,1536]{1,0:T(8,128)S(1)}, u32[]{:S(2)}) copy-start(f32[48,1536]{1,0:T(8,128)S(1)} %collective-permute-done.4.refs_8_) | copy-start | bytes 884740
  23.8 31.7 %copy-start.59 = (f32[48,1536]{1,0:T(8,128)}, f32[48,1536]{1,0:T(8,128)S(1)}, u32[]{:S(2)}) copy-start(f32[48,1536]{1,0:T(8,128)S(1)} %collective-permute-done.5.refs_9_) | copy-start | bytes 884740
  32.6 22.9 %copy-start.60 = (f32[48,1536]{1,0:T(8,128)}, f32[48,1536]{1,0:T(8,128)S(1)}, u32[]{:S(2)}) copy-start(f32[48,1536]{1,0:T(8,128)S(1)} %collective-permute-done.3.refs_2_) | copy-start | bytes 884740
  32.6 22.8 %copy-start.61 = (f32[48,1536]{1,0:T(8,128)}, f32[48,1536]{1,0:T(8,128)S(1)}, u32[]{:S(2)}) copy-start(f32[48,1536]{1,0:T(8,128)S(1)} %collective-permute-done.2.refs_5_) | copy-start | bytes 884740
  32.6 1.9 collective-permute-start.9
  32.7 11.2 %collective-permute-start.7 = (f32[48,1536]{1,0:T(8,128)S(1)}, f32[48,1536]{1,0:T(8,128)S(1)}, u32[]{:S(2)}, u32[]{:S(2)}) collective-permute-start(f32[48,1536]{1,0:T(8,128)S(1)} %collective-permute-done.3.refs_2_), channel_id=1, source_target_pairs={{0,2},{2,4},{4,6},{6,0},{1,3},{3,5},{5,7},{7,1},{8,10},{10,12},{12... | collective-permute-start | bytes 884744 | tf_op jit(solution)/shard_map/ppermute | solution.py:71
  33.0 10.8 %collective-permute-start.6 = (f32[48,1536]{1,0:T(8,128)S(1)}, f32[48,1536]{1,0:T(8,128)S(1)}, u32[]{:S(2)}, u32[]{:S(2)}) collective-permute-start(f32[48,1536]{1,0:T(8,128)S(1)} %collective-permute-done.3.refs_2_), channel_id=1, source_target_pairs={{0,16},{8,24},{16,0},{24,8},{1,17},{9,25},{17,1},{25,9},{2,18},{10... | collective-permute-start | bytes 884744 | tf_op jit(solution)/shard_map/ppermute | solution.py:67
  34.5 11.8 %collective-permute-start.11 = (f32[48,1536]{1,0:T(8,128)S(1)}, f32[48,1536]{1,0:T(8,128)}, u32[]{:S(2)}, u32[]{:S(2)}) collective-permute-start(f32[48,1536]{1,0:T(8,128)S(1)} %collective-permute-done.3.refs_2_), channel_id=1, source_target_pairs={{0,8},{8,0},{16,24},{24,16},{1,9},{9,1},{17,25},{25,17},{2,10},{10... | collective-permute-start | bytes 884744 | tf_op jit(solution)/shard_map/ppermute | solution.py:63
  34.5 20.9 %copy-start.62 = (f32[48,1536]{1,0:T(8,128)}, f32[48,1536]{1,0:T(8,128)S(1)}, u32[]{:S(2)}) copy-start(f32[48,1536]{1,0:T(8,128)S(1)} %collective-permute-done.8.refs_10_) | copy-start | bytes 884740
  34.6 20.9 %copy-start.63 = (f32[48,1536]{1,0:T(8,128)}, f32[48,1536]{1,0:T(8,128)S(1)}, u32[]{:S(2)}) copy-start(f32[48,1536]{1,0:T(8,128)S(1)} %collective-permute-done.9.refs_11_) | copy-start | bytes 884740
  43.9 2.5 collective-permute-start.12
  44.0 9.5 %collective-permute-start.10 = (f32[48,1536]{1,0:T(8,128)S(1)}, f32[48,1536]{1,0:T(8,128)}, u32[]{:S(2)}, u32[]{:S(2)}) collective-permute-start(f32[48,1536]{1,0:T(8,128)S(1)} %collective-permute-done.7.refs_3_), channel_id=1, source_target_pairs={{0,16},{8,24},{16,0},{24,8},{1,17},{9,25},{17,1},{25,9},{2,18},{10... | collective-permute-start | bytes 884744 | tf_op jit(solution)/shard_map/ppermute | solution.py:67
  46.2 9.2 %collective-permute-start.13 = (f32[48,1536]{1,0:T(8,128)S(1)}, f32[48,1536]{1,0:T(8,128)}, u32[]{:S(2)}, u32[]{:S(2)}) collective-permute-start(f32[48,1536]{1,0:T(8,128)S(1)} %collective-permute-done.7.refs_3_), channel_id=1, source_target_pairs={{0,8},{8,0},{16,24},{24,16},{1,9},{9,1},{17,25},{25,17},{2,10},{10... | collective-permute-start | bytes 884744 | tf_op jit(solution)/shard_map/ppermute | solution.py:63
  53.5 2.0 collective-permute-start.14
  64.0 15.5 %copy-start.71 = (f32[512]{0:T(512)}, f32[512]{0:T(512)S(1)}, u32[]{:S(2)}) copy-start(f32[512]{0:T(512)S(1)} %get-tuple-element.163) | copy-start | bytes 6148
  64.0 41.9 %copy-start.76 = (f32[512]{0:T(512)}, f32[512]{0:T(512)S(1)}, u32[]{:S(2)}) copy-start(f32[512]{0:T(512)S(1)} %get-tuple-element.162) | copy-start | bytes 6148
  81.8 21.4 %collective-permute-start.18 = (f32[6,65,128]{2,1,0:T(8,128)S(1)}, f32[6,65,128]{2,1,0:T(8,128)S(1)}, u32[]{:S(2)}, u32[]{:S(2)}) collective-permute-start(f32[6,65,128]{2,1,0:T(8,128)S(1)} %pad_maximum_fusion.12), channel_id=1, source_target_pairs={{0,8},{2,10},{4,12},{6,14},{8,16},{10,18},{12,20},{14,22},{16,24},... | collective-permute-start | bytes 599048 | tf_op jit(solution)/shard_map/ppermute | solution.py:176
  84.2 18.9 %collective-permute-start.17 = (f32[6,65,128]{2,1,0:T(8,128)S(1)}, f32[6,65,128]{2,1,0:T(8,128)S(1)}, u32[]{:S(2)}, u32[]{:S(2)}) collective-permute-start(f32[6,65,128]{2,1,0:T(8,128)S(1)} %pad_maximum_fusion.12), channel_id=1, source_target_pairs={{0,6},{2,8},{4,10},{6,12},{8,14},{10,16},{12,18},{14,20},{16,22},{... | collective-permute-start | bytes 599048 | tf_op jit(solution)/shard_map/ppermute | solution.py:176
  87.8 15.4 %collective-permute-start.16 = (f32[6,65,128]{2,1,0:T(8,128)S(1)}, f32[6,65,128]{2,1,0:T(8,128)S(1)}, u32[]{:S(2)}, u32[]{:S(2)}) collective-permute-start(f32[6,65,128]{2,1,0:T(8,128)S(1)} %pad_maximum_fusion.12), channel_id=1, source_target_pairs={{0,4},{2,6},{4,8},{6,10},{8,12},{10,14},{12,16},{14,18},{16,20},{1... | collective-permute-start | bytes 599048 | tf_op jit(solution)/shard_map/ppermute | solution.py:176
  89.1 14.1 %collective-permute-start.15 = (f32[6,65,128]{2,1,0:T(8,128)S(1)}, f32[6,65,128]{2,1,0:T(8,128)S(1)}, u32[]{:S(2)}, u32[]{:S(2)}) collective-permute-start(f32[6,65,128]{2,1,0:T(8,128)S(1)} %pad_maximum_fusion.12), channel_id=1, source_target_pairs={{0,2},{2,4},{4,6},{6,8},{8,10},{10,12},{12,14},{14,16},{16,18},{18... | collective-permute-start | bytes 599048 | tf_op jit(solution)/shard_map/ppermute | solution.py:176
  113.2 25.7 %collective-permute-start.19 = (f32[512,768]{1,0:T(8,128)}, f32[512,768]{1,0:T(8,128)}, u32[]{:S(2)}, u32[]{:S(2)}) collective-permute-start(f32[512,768]{1,0:T(8,128)} %fusion.71), channel_id=1, source_target_pairs={{0,1},{1,0},{2,3},{3,2},{4,5},{5,4},{6,7},{7,6},{8,9},{9,8},{10,11... | collective-permute-start | bytes 4718600 | tf_op jit(solution)/shard_map/ppermute | solution.py:31
  115.5 23.4 %copy-start.90 = (f32[768]{0:T(1024)S(1)}, f32[768]{0:T(1024)}, u32[]{:S(2)}) copy-start(f32[768]{0:T(1024)} %param.26) | copy-start | bytes 9220
  115.5 66.8 %all-to-all-start = ((f32[8,64,768]{2,1,0:T(8,128)}), f32[8,64,768]{2,1,0:T(8,128)}, u32[]{:S(2)}, u32[]{:S(2)}) async-start(f32[8,64,768]{2,1,0:T(8,128)} %bitcast.208), calls=%async_computation | async-start | bytes 3145728 | tf_op jit(solution)/shard_map/all_to_all | solution.py:298
  133.8 315.4 %reduce-scatter.2.cloned.1.call-start = ((), (), s32[]{:S(2)}) async-start(), calls=%async_computation.4 | async-start | bytes 10027008 | tf_op jit(solution)/shard_map/reduce_scatter | solution.py:51
  195.5 21.1 %copy-start.100 = (f32[512,1536]{1,0:T(8,128)}, f32[512,1536]{1,0:T(8,128)S(1)}, u32[]{:S(2)}) copy-start(f32[512,1536]{1,0:T(8,128)S(1)} %fusion.24) | copy-start | bytes 9437188
  209.1 36.6 %collective-permute-start.20 = (f32[512,768]{1,0:T(8,128)}, f32[512,768]{1,0:T(8,128)}, u32[]{:S(2)}, u32[]{:S(2)}) collective-permute-start(f32[512,768]{1,0:T(8,128)} %fusion.10), channel_id=1, source_target_pairs={{0,1},{1,0},{2,3},{3,2},{4,5},{5,4},{6,7},{7,6},{8,9},{9,8},{10,11... | collective-permute-start | bytes 4718600 | tf_op jit(solution)/shard_map/ppermute | solution.py:31
  250.8 16.7 %slice-start.2 = ((s8[9437184]{0:T(1024)(128)(4,1)}), s8[1048576]{0:T(1024)(128)(4,1)S(1)}, s32[]{:S(2)}) async-start(s8[9437184]{0:T(1024)(128)(4,1)} %bitcast.206), calls=%async_computation.7 | async-start | bytes 2097152
  255.5 22.4 %copy-start.21 = (f32[512,384]{0,1:T(8,128)}, f32[512,384]{0,1:T(8,128)S(1)}, u32[]{:S(2)}) copy-start(f32[512,384]{0,1:T(8,128)S(1)} %fusion.69) | copy-start | bytes 2359300
  257.2 20.7 %copy-start.66 = (f32[6,512]{1,0:T(8,128)}, f32[6,512]{1,0:T(8,128)S(1)}, u32[]{:S(2)}) copy-start(f32[6,512]{1,0:T(8,128)S(1)} %negate_divide_fusion) | copy-start | bytes 36868
  258.1 44.8 %collective-permute-start.24 = (f32[6,65,128]{2,1,0:T(8,128)}, f32[6,65,128]{2,1,0:T(8,128)}, u32[]{:S(2)}, u32[]{:S(2)}) collective-permute-start(f32[6,65,128]{2,1,0:T(8,128)} %pad_maximum_fusion.13), channel_id=1, source_target_pairs={{8,0},{10,2},{12,4},{14,6},{16,8},{18,10},{20,12},{22,14},{24,16},... | collective-permute-start | bytes 599048 | tf_op jit(solution)/shard_map/ppermute | solution.py:176
  259.7 43.3 %collective-permute-start.23 = (f32[6,65,128]{2,1,0:T(8,128)}, f32[6,65,128]{2,1,0:T(8,128)}, u32[]{:S(2)}, u32[]{:S(2)}) collective-permute-start(f32[6,65,128]{2,1,0:T(8,128)} %pad_maximum_fusion.13), channel_id=1, source_target_pairs={{6,0},{8,2},{10,4},{12,6},{14,8},{16,10},{18,12},{20,14},{22,16},{... | collective-permute-start | bytes 599048 | tf_op jit(solution)/shard_map/ppermute | solution.py:176
  261.2 41.7 %collective-permute-start.22 = (f32[6,65,128]{2,1,0:T(8,128)}, f32[6,65,128]{2,1,0:T(8,128)}, u32[]{:S(2)}, u32[]{:S(2)}) collective-permute-start(f32[6,65,128]{2,1,0:T(8,128)} %pad_maximum_fusion.13), channel_id=1, source_target_pairs={{4,0},{6,2},{8,4},{10,6},{12,8},{14,10},{16,12},{18,14},{20,16},{2... | collective-permute-start | bytes 599048 | tf_op jit(solution)/shard_map/ppermute | solution.py:176
  262.5 40.4 %collective-permute-start.21 = (f32[6,65,128]{2,1,0:T(8,128)}, f32[6,65,128]{2,1,0:T(8,128)}, u32[]{:S(2)}, u32[]{:S(2)}) collective-permute-start(f32[6,65,128]{2,1,0:T(8,128)} %pad_maximum_fusion.13), channel_id=1, source_target_pairs={{2,0},{4,2},{6,4},{8,6},{10,8},{12,10},{14,12},{16,14},{18,16},{20... | collective-permute-start | bytes 599048 | tf_op jit(solution)/shard_map/ppermute | solution.py:176
  273.7 32.9 %collective-permute-start.25 = (f32[8,32,768]{2,1,0:T(8,128)}, f32[8,32,768]{2,1,0:T(8,128)}, u32[]{:S(2)}, u32[]{:S(2)}) collective-permute-start(f32[8,32,768]{2,1,0:T(8,128)} %constant_dynamic-slice_fusion.1), channel_id=1, source_target_pairs={{0,1},{1,0},{2,3},{3,2},{4,5},{5,4},{6,7},{7,6},{8,9},{9,8},{10,11... | collective-permute-start | bytes 2359304 | tf_op jit(solution)/shard_map/ppermute | solution.py:344
  314.5 53.0 %all-to-all-start.1 = ((f32[8,32,768]{2,1,0:T(8,128)}), f32[8,32,768]{2,1,0:T(8,128)}, u32[]{:S(2)}, u32[]{:S(2)}) async-start(f32[8,32,768]{2,1,0:T(8,128)} %broadcast_select_fusion), calls=%async_computation.1 | async-start | bytes 1572864 | tf_op jit(solution)/shard_map/all_to_all | solution.py:371
  343.0 20.9 %collective-permute-start.26 = (f32[2,4,48,1536]{3,2,1,0:T(8,128)}, f32[2,4,48,1536]{3,2,1,0:T(8,128)}, u32[]{:S(2)}, u32[]{:S(2)}) collective-permute-start(f32[2,4,48,1536]{3,2,1,0:T(8,128)} %dynamic-slice_bitcast_fusion), channel_id=1, source_target_pairs={{0,8},{8,0},{16,24},{24,16},{1,9},{9,1},{17,25},{25,17},{2,10},{10... | collective-permute-start | bytes 7077896 | tf_op jit(solution)/shard_map/ppermute | solution.py:63
  358.8 3.7 collective-permute-start.31
  364.0 8.6 %collective-permute-start.32 = (f32[448,128]{1,0:T(8,128)}, f32[448,128]{1,0:T(8,128)}, u32[]{:S(2)}, u32[]{:S(2)}) collective-permute-start(f32[448,128]{1,0:T(8,128)} %pad_bitcast_fusion), channel_id=1, source_target_pairs={{0,8},{8,0},{16,24},{24,16},{1,9},{9,1},{17,25},{25,17},{2,10},{10... | collective-permute-start | bytes 688136 | tf_op jit(solution)/shard_map/ppermute | solution.py:63
  371.1 27.8 %collective-permute-start.27 = (f32[4,48,1024]{2,1,0:T(8,128)}, f32[4,48,1024]{2,1,0:T(8,128)}, u32[]{:S(2)}, u32[]{:S(2)}) collective-permute-start(f32[4,48,1024]{2,1,0:T(8,128)} %dynamic-slice_bitcast_fusion.1), channel_id=1, source_target_pairs={{0,16},{8,24},{16,0},{24,8},{1,17},{9,25},{17,1},{25,9},{2,18},{10... | collective-permute-start | bytes 2359304 | tf_op jit(solution)/shard_map/ppermute | solution.py:67
  374.2 22.0 %collective-permute-start.33 = (f32[448,128]{1,0:T(8,128)}, f32[448,128]{1,0:T(8,128)}, u32[]{:S(2)}, u32[]{:S(2)}) collective-permute-start(f32[448,128]{1,0:T(8,128)} %fusion.138), channel_id=1, source_target_pairs={{0,16},{8,24},{16,0},{24,8},{1,17},{9,25},{17,1},{25,9},{2,18},{10... | collective-permute-start | bytes 688136 | tf_op jit(solution)/shard_map/ppermute | solution.py:67
  375.4 22.3 %copy-start.43 = (f32[56576]{0:T(1024)S(1)}, f32[56576]{0:T(1024)}, u32[]{:S(2)}) copy-start(f32[56576]{0:T(1024)} %copy-done.41) | copy-start | bytes 678916
  376.7 22.2 %copy-start.34 = (f32[2,4,48,1024]{3,2,1,0:T(8,128)S(1)}, f32[2,4,48,1024]{3,2,1,0:T(8,128)}, u32[]{:S(2)}) copy-start(f32[2,4,48,1024]{3,2,1,0:T(8,128)} %copy-done.33) | copy-start | bytes 4718596
  376.8 22.0 %collective-permute-start.28 = (f32[2,48,512]{2,1,0:T(8,128)S(1)}, f32[2,48,512]{2,1,0:T(8,128)S(1)}, u32[]{:S(2)}, u32[]{:S(2)}) collective-permute-start(f32[2,48,512]{2,1,0:T(8,128)S(1)} %get-tuple-element.141), channel_id=1, source_target_pairs={{0,2},{2,4},{4,6},{6,0},{1,3},{3,5},{5,7},{7,1},{8,10},{10,12},{12... | collective-permute-start | bytes 589832 | tf_op jit(solution)/shard_map/ppermute | solution.py:125
  379.8 19.0 %collective-permute-start.30 = (f32[2,48,512]{2,1,0:T(8,128)S(1)}, f32[2,48,512]{2,1,0:T(8,128)S(1)}, u32[]{:S(2)}, u32[]{:S(2)}) collective-permute-start(f32[2,48,512]{2,1,0:T(8,128)S(1)} %get-tuple-element.142), channel_id=1, source_target_pairs={{0,6},{2,0},{4,2},{6,4},{1,7},{3,1},{5,3},{7,5},{8,14},{10,8},{12,... | collective-permute-start | bytes 589832 | tf_op jit(solution)/shard_map/ppermute | solution.py:125
  380.7 18.1 %collective-permute-start.29 = (f32[2,48,512]{2,1,0:T(8,128)S(1)}, f32[2,48,512]{2,1,0:T(8,128)S(1)}, u32[]{:S(2)}, u32[]{:S(2)}) collective-permute-start(f32[2,48,512]{2,1,0:T(8,128)S(1)} %get-tuple-element.143), channel_id=1, source_target_pairs={{0,4},{2,6},{4,0},{6,2},{1,5},{3,7},{5,1},{7,3},{8,12},{10,14},{12... | collective-permute-start | bytes 589832 | tf_op jit(solution)/shard_map/ppermute | solution.py:125
  396.2 37.1 %collective-permute-start.40 = (f32[512,768]{1,0:T(8,128)S(1)}, f32[512,768]{1,0:T(8,128)S(1)}, u32[]{:S(2)}, u32[]{:S(2)}) collective-permute-start(f32[512,768]{1,0:T(8,128)S(1)} %get-tuple-element.73), channel_id=1, source_target_pairs={{0,1},{1,0},{2,3},{3,2},{4,5},{5,4},{6,7},{7,6},{8,9},{9,8},{10,11... | collective-permute-start | bytes 4718600 | tf_op jit(solution)/shard_map/ppermute | solution.py:143
  400.2 7.3 %collective-permute-start.37 = (f32[48,512]{1,0:T(8,128)S(1)}, f32[48,512]{1,0:T(8,128)S(1)}, u32[]{:S(2)}, u32[]{:S(2)}) collective-permute-start(f32[48,512]{1,0:T(8,128)S(1)} %dynamic-slice_bitcast_fusion.8), channel_id=1, source_target_pairs={{0,16},{8,24},{16,0},{24,8},{1,17},{9,25},{17,1},{25,9},{2,18},{10... | collective-permute-start | bytes 294920 | tf_op jit(solution)/shard_map/ppermute | solution.py:67
  401.2 22.2 %collective-permute-start.38 = (f32[448,128]{1,0:T(8,128)S(1)}, f32[448,128]{1,0:T(8,128)S(1)}, u32[]{:S(2)}, u32[]{:S(2)}) collective-permute-start(f32[448,128]{1,0:T(8,128)S(1)} %fusion.175), channel_id=1, source_target_pairs={{0,2},{2,0},{4,6},{6,4},{1,3},{3,1},{5,7},{7,5},{8,10},{10,8},{12,... | collective-permute-start | bytes 688136 | tf_op jit(solution)/shard_map/ppermute | solution.py:149
  403.6 12.3 %collective-permute-start.34 = (f32[48,1024]{1,0:T(8,128)S(1)}, f32[48,1024]{1,0:T(8,128)S(1)}, u32[]{:S(2)}, u32[]{:S(2)}) collective-permute-start(f32[48,1024]{1,0:T(8,128)S(1)} %get-tuple-element.138), channel_id=1, source_target_pairs={{0,2},{2,4},{4,6},{6,0},{1,3},{3,5},{5,7},{7,1},{8,10},{10,12},{12... | collective-permute-start | bytes 589832 | tf_op jit(solution)/shard_map/ppermute | solution.py:125
  403.7 16.9 %collective-permute-start.36 = (f32[48,1024]{1,0:T(8,128)S(1)}, f32[48,1024]{1,0:T(8,128)S(1)}, u32[]{:S(2)}, u32[]{:S(2)}) collective-permute-start(f32[48,1024]{1,0:T(8,128)S(1)} %get-tuple-element.139), channel_id=1, source_target_pairs={{0,6},{2,0},{4,2},{6,4},{1,7},{3,1},{5,3},{7,5},{8,14},{10,8},{12,... | collective-permute-start | bytes 589832 | tf_op jit(solution)/shard_map/ppermute | solution.py:125
  407.5 15.8 %collective-permute-start.35 = (f32[48,1024]{1,0:T(8,128)S(1)}, f32[48,1024]{1,0:T(8,128)S(1)}, u32[]{:S(2)}, u32[]{:S(2)}) collective-permute-start(f32[48,1024]{1,0:T(8,128)S(1)} %get-tuple-element.140), channel_id=1, source_target_pairs={{0,4},{2,6},{4,0},{6,2},{1,5},{3,7},{5,1},{7,3},{8,12},{10,14},{12... | collective-permute-start | bytes 589832 | tf_op jit(solution)/shard_map/ppermute | solution.py:125
  423.4 9.9 %collective-permute-start.39 = (f32[448,128]{1,0:T(8,128)S(1)}, f32[448,128]{1,0:T(8,128)S(1)}, u32[]{:S(2)}, u32[]{:S(2)}) collective-permute-start(f32[448,128]{1,0:T(8,128)S(1)} %add.627), channel_id=1, source_target_pairs={{0,4},{2,6},{4,0},{6,2},{1,5},{3,7},{5,1},{7,3},{8,12},{10,14},{12... | collective-permute-start | bytes 688136 | tf_op jit(solution)/shard_map/ppermute | solution.py:151
  (88 other events, 460.5 us)
Sparse Core Ops, SparseCore 0:
  60.6 104.4 all-gather.1
  230.0 134.8 reduce-scatter.1
